TPU v7x, 32 devices: a whole 2x2x4 slice. The times are simulated.
32 devices in a mesh: depth: 8 (over z, x), gx: 4 (over y, core).
Axes of the slice: x: 2, y: 2, z: 4, core: 2. Of those that a mesh axis runs over, the one named last changes fastest.
Arguments:
- volume: bfloat16 [64, 192, 2, 512], P(None, 'depth', None, 'gx'), may hold values from -6 to 6
- conv_first: bfloat16 [3, 3, 3, 64, 64], replicated, may hold values from -0.15625 to 0.15625
- conv_second: bfloat16 [3, 3, 3, 64, 64], replicated, may hold values from -0.15625 to 0.15625
- mode_weights: bfloat16 [64, 64, 64], P('depth'), may hold values from -0.75 to 0.75
Outputs:
- next_volume: bfloat16 [64, 192, 2, 512], P(None, 'depth', None, 'gx')
All inputs are finite; a program needn't handle non-finite values.
Results may differ from a plain program's by a relative error of at most 0.01.
Values may be sent and summed in bfloat16 or wider, within the bound.
No kernel may reach another device: no remote copies, remote signals or barrier semaphores. Data moves between devices by JAX's collectives and lax.ppermute only.
A program may use at most 64 MiB of HBM per device.

v0:
```python
import functools
import math

import jax
import jax.numpy as jnp
from jax import lax
from jax.experimental import pallas as pl
from jax.experimental.pallas import tpu as pltpu
from jax.sharding import PartitionSpec as P


MODES = 32
BF = jnp.bfloat16
F32 = jnp.float32
VMEM = pl.BlockSpec(memory_space=pltpu.VMEM)


def mode_basis(mode_index, depth_pos, total_z):
    frequency = jnp.where(mode_index < MODES, mode_index, mode_index - MODES + 1).astype(F32)
    odd_steps = (2 * depth_pos + 1).astype(F32)
    angles = frequency[:, None] * odd_steps[None, :] * (math.pi / (2.0 * total_z))
    values = jnp.where((mode_index < MODES)[:, None], jnp.cos(angles), jnp.sin(angles))
    return (values * math.sqrt(2.0 / total_z)).astype(BF)


def cost(flops, nbytes, trans=0):
    return pl.CostEstimate(flops=flops, bytes_accessed=nbytes, transcendentals=trans)


def params():
    return pltpu.CompilerParams(vmem_limit_bytes=20 * 1024 * 1024)


def target(n, k):
    me = lax.axis_index("depth")
    return me ^ k if n & (n - 1) == 0 else (me + k) % n


def split_kernel(slab, flat, weights, vt, *refs):
    *chunks, wide = refs
    pairs, cols, lanes = vt.shape
    n = len(chunks)
    part = cols // n
    half = lanes // 2
    own = weights.shape[0] // 2
    ch = weights.shape[2]
    stride = flat.shape[0] // ch
    ny = stride // slab
    core = lax.axis_index("gx") % 2
    wide[...] = flat[...].astype(F32)
    for q in range(pairs):
        rows = [wide[pl.ds(2 * q * ny + j, ch, stride=stride), :] for j in range(2 * ny)]
        vt[q] = jnp.concatenate(rows, axis=0).astype(BF).T
    body = 2 * pairs * part
    for k in range(n):
        start = pl.multiple_of(target(n, k) * part, part)
        for q in range(pairs):
            for par in range(2):
                chunks[k][pl.ds((par * pairs + q) * part, part), :] = vt[
                    q, pl.ds(start, part), pl.ds(par * half, half)
                ]
        for j in range(own // 2):
            first = weights[core * own + 2 * j]
            second = weights[core * own + 2 * j + 1]
            chunks[k][pl.ds(body + j * ch, ch), :] = jnp.concatenate([first, second], axis=1)


def taps_kernel(first, second, out_first, out_second):
    ch = first.shape[3]
    for src, dst in ((first, out_first), (second, out_second)):
        for e in range(3):
            block = {}
            for a in range(3):
                for yi in range(2):
                    both = jnp.concatenate([src[a, yi + 1, e], src[a, yi, e]], axis=0)
                    block[a, yi] = both.astype(F32).T.astype(BF)
            for h in range(2):
                for pi in range(2):
                    for po in range(2):
                        a = 2 * h + pi - po
                        for yi in range(2):
                            value = block[a, yi] if 0 <= a <= 2 else jnp.zeros((ch, 2 * ch), BF)
                            dst[
                                e * 2 + h,
                                pl.ds((pi * 2 + yi) * ch, ch),
                                pl.ds(po * 2 * ch, 2 * ch),
                            ] = value


def shifted(dst, index, rows, value):
    n = value.shape[0]
    wide = value.astype(F32)
    dst[1, pl.ds(index * rows, rows), :] = value
    dst[0, pl.ds(index * rows, rows), :] = pltpu.roll(wide, 1, 0).astype(BF)
    dst[2, pl.ds(index * rows, rows), :] = pltpu.roll(wide, n - 1, 0).astype(BF)


def conv_kernel(ngx, n, flat, vt, before, after, left, right, w1, w2, out, ext, hid):
    pairs, cols, lanes = vt.shape
    rows = cols + 16
    stride = 4 * flat.shape[0] // lanes
    ch = lanes // 4
    me = lax.axis_index("depth")
    gx = lax.axis_index("gx")
    fill = jnp.zeros((rows - cols - 4, lanes), F32)
    for q in range(pairs + 2):
        if 0 < q < pairs + 1:
            mid, lo, hi = vt[q - 1], left[q - 1], right[q - 1]
        else:
            end = before if q == 0 else after
            mid, lo, hi = end[pl.ds(0, cols), :], end[pl.ds(cols + 2, 2), :], end[pl.ds(cols, 2), :]
        ring = jnp.concatenate(
            [mid.astype(F32), hi.astype(F32), fill, lo.astype(F32)], axis=0
        ).astype(BF)
        shifted(ext, q, rows, ring)
    at = lax.broadcasted_iota(jnp.int32, (rows, lanes), 0)
    lane = lax.broadcasted_iota(jnp.int32, (rows, lanes), 1)
    inside = jnp.logical_and(
        jnp.logical_or(at != rows - 1, gx > 0), jnp.logical_or(at != cols, gx < ngx - 1)
    )
    for p in range(pairs + 1):
        acc = jnp.zeros((rows, lanes), F32)
        for e in range(3):
            for h in range(2):
                acc += jnp.dot(
                    ext[e, pl.ds((p + h) * rows, rows), :],
                    w1[e * 2 + h],
                    preferred_element_type=F32,
                )
        keep = inside
        if p == 0:
            keep = jnp.logical_and(keep, jnp.logical_or(lane >= lanes // 2, me > 0))
        if p == pairs:
            keep = jnp.logical_and(keep, jnp.logical_or(lane < lanes // 2, me < n - 1))
        value = jnp.where(keep, jax.nn.gelu(acc), 0.0).astype(BF)
        shifted(hid, p, rows, value)
    for p in range(pairs):
        acc = jnp.zeros((cols, lanes), F32)
        for e in range(3):
            for h in range(2):
                acc += jnp.dot(
                    hid[e, pl.ds((p + h) * rows, cols), :],
                    w2[e * 2 + h],
                    preferred_element_type=F32,
                )
        turned = acc.T
        for j in range(4):
            out[pl.ds(4 * p + j, ch, stride=stride), :] = turned[j * ch : (j + 1) * ch]
    out[...] += flat[...].astype(F32)


def spectral_kernel(basis, basis_t, other, *refs):
    n = other.shape[0]
    chunks, outs = refs[:n], refs[n : 2 * n]
    field, coef, mix = refs[2 * n :]
    modes = basis.shape[0]
    wide = other.shape[2]
    ch = wide // 2
    per = field.shape[1] // n
    body = 2 * per
    steps = basis.shape[1] // 2
    part = field.shape[1] // steps
    for k in range(n):
        for par in range(2):
            field[par, pl.ds(k * per, per), :] = chunks[k][pl.ds(par * per, per), :].astype(F32)
    for x in range(part):
        piece = jnp.concatenate(
            [field[par, pl.ds(x, steps, stride=part), :].astype(BF) for par in range(2)], axis=0
        )
        coef[pl.ds(x, modes, stride=part), :] = jnp.dot(
            basis[...], piece, preferred_element_type=F32
        )
    low = lax.broadcasted_iota(jnp.int32, (part, wide), 1) < ch
    duo = modes // 2 // (2 * n)
    at = 0
    for side in range(2):
        for k in range(n):
            for j in range(duo):
                if side == 0:
                    w = chunks[k][pl.ds(body + j * ch, ch), :]
                else:
                    w = other[k, pl.ds(j * ch, ch), :]
                c0 = coef[pl.ds(at * part, part), :]
                c1 = coef[pl.ds((at + 1) * part, part), :]
                lhs = jnp.concatenate(
                    [
                        jnp.where(low, c0, 0.0),
                        jnp.where(low, pltpu.roll(c0, ch, 1), 0.0),
                        jnp.where(low, 0.0, pltpu.roll(c1, ch, 1)),
                        jnp.where(low, 0.0, c1),
                    ],
                    axis=0,
                ).astype(BF)
                r = lax.dot_general(
                    lhs, w, (((1,), (1,)), ((), ())), preferred_element_type=F32
                )
                for t in range(2):
                    mix[pl.ds((at + t) * part, part), :] = jnp.concatenate(
                        [
                            r[2 * t * part : (2 * t + 1) * part],
                            r[(2 * t + 1) * part : (2 * t + 2) * part],
                        ],
                        axis=1,
                    )
                at += 2
    for x in range(part):
        value = jnp.dot(
            basis_t[...],
            mix[pl.ds(x, modes, stride=part), :].astype(BF),
            preferred_element_type=F32,
        )
        for par in range(2):
            field[par, pl.ds(x, steps, stride=part), :] = value[par * steps : (par + 1) * steps]
    for k in range(n):
        for par in range(2):
            outs[k][pl.ds(par * per, per), :] = field[par, pl.ds(k * per, per), :].astype(BF)


def join_kernel(base, *refs):
    *chunks, out, total, wide = refs
    pairs, cols, lanes = total.shape
    n = len(chunks)
    part = cols // n
    half = lanes // 2
    stride = 4 * base.shape[0] // lanes
    ch = lanes // 4
    for k in range(n):
        start = pl.multiple_of(target(n, k) * part, part)
        for q in range(pairs):
            for par in range(2):
                total[q, pl.ds(start, part), pl.ds(par * half, half)] = chunks[k][
                    pl.ds((par * pairs + q) * part, part), :
                ]
    for q in range(pairs):
        turned = total[q].T.astype(F32)
        for j in range(4):
            wide[pl.ds(4 * q + j, ch, stride=stride), :] = turned[j * ch : (j + 1) * ch]
    out[...] = (base[...] + wide[...]).astype(BF)


def shift_line(value, axis, step):
    count = lax.axis_size(axis)
    pairs = [(i, i + step) for i in range(count) if 0 <= i + step < count]
    return lax.ppermute(value, axis, pairs)


def block(volume, conv_first, conv_second, mode_weights):
    ch, slab, ny, cols = volume.shape
    n = lax.axis_size("depth")
    ngx = lax.axis_size("gx")
    total_z = slab * n
    pairs = slab // 2
    lanes = 2 * ny * ch
    part = cols // n
    per = pairs * part
    modes = mode_weights.shape[0] * n
    me = lax.axis_index("depth")
    core = lax.axis_index("gx") % 2
    own = mode_weights.shape[0] // 2
    twofold = n & (n - 1) == 0
    ks = jnp.arange(n, dtype=jnp.int32)
    source = me ^ ks if twofold else (me - ks) % n

    def send(value, k, back=False):
        if k == 0:
            return value
        if twofold:
            table = [(i, i ^ k) for i in range(n)]
        else:
            table = [(i, (i - k if back else i + k) % n) for i in range(n)]
        return lax.ppermute(value, "depth", table)

    flat = volume.reshape(ch * slab * ny, cols)
    wrows = own // 2 * ch
    vt, *chunks = pl.pallas_call(
        functools.partial(split_kernel, slab),
        out_shape=[jax.ShapeDtypeStruct((pairs, cols, lanes), BF)]
        + [jax.ShapeDtypeStruct((2 * per + wrows, lanes // 2), BF)] * n,
        in_specs=[VMEM, VMEM],
        out_specs=[VMEM] * (n + 1),
        scratch_shapes=[pltpu.VMEM(flat.shape, F32)],
        compiler_params=params(),
        cost_estimate=cost(0, 3 * volume.size * 2),
    )(flat, mode_weights)
    got = [send(chunks[k], k) for k in range(n)]

    left = shift_line(vt[:, cols - 2 :], "gx", 1)
    right = shift_line(vt[:, :2], "gx", -1)
    last = jnp.concatenate([vt[pairs - 1], right[pairs - 1], left[pairs - 1]], axis=0)
    before = shift_line(last, "depth", 1)
    first = jnp.concatenate([vt[0], right[0], left[0]], axis=0)
    after = shift_line(first, "depth", -1)

    w1, w2 = pl.pallas_call(
        taps_kernel,
        out_shape=[jax.ShapeDtypeStruct((6, lanes, lanes), BF)] * 2,
        in_specs=[VMEM, VMEM],
        out_specs=[VMEM, VMEM],
        compiler_params=params(),
        cost_estimate=cost(0, 4 * conv_first.size * 2 * 4),
    )(conv_first, conv_second)

    mine = jnp.stack([g[2 * per :] for g in got])
    other = lax.ppermute(mine, "gx", [(i, i ^ 1) for i in range(ngx)])
    inner = jnp.arange(own, dtype=jnp.int32)[None, :] + source[:, None] * (2 * own)
    ids = jnp.concatenate(
        [(inner + core * own).reshape(-1), (inner + (1 - core) * own).reshape(-1)]
    )
    depth_pos = (
        jnp.arange(2, dtype=jnp.int32)[:, None, None]
        + source[None, :, None] * slab
        + 2 * jnp.arange(pairs, dtype=jnp.int32)[None, None, :]
    ).reshape(-1)
    basis = mode_basis(ids, depth_pos, total_z)
    outs = pl.pallas_call(
        spectral_kernel,
        out_shape=[jax.ShapeDtypeStruct((2 * per, lanes // 2), BF)] * n,
        in_specs=[VMEM] * (3 + n),
        out_specs=[VMEM] * n,
        scratch_shapes=[
            pltpu.VMEM((2, n * per, lanes // 2), F32),
            pltpu.VMEM((modes * part, lanes // 2), F32),
            pltpu.VMEM((modes * part, lanes // 2), F32),
        ],
        compiler_params=params(),
        cost_estimate=cost(4 * modes * total_z * part * lanes // 2, 3 * volume.size * 2),
    )(basis, basis.T, other, *got)
    spec = [send(outs[k], k, True) for k in range(n)]

    base = pl.pallas_call(
        functools.partial(conv_kernel, ngx, n),
        out_shape=jax.ShapeDtypeStruct(flat.shape, F32),
        in_specs=[VMEM] * 8,
        out_specs=VMEM,
        scratch_shapes=[
            pltpu.VMEM((3, (pairs + 2) * (cols + 16), lanes), BF),
            pltpu.VMEM((3, (pairs + 1) * (cols + 16), lanes), BF),
        ],
        compiler_params=params(),
        cost_estimate=cost(4 * 6 * pairs * cols * lanes * lanes, volume.size * 8),
    )(flat, vt, before, after, left, right, w1, w2)

    out = pl.pallas_call(
        join_kernel,
        out_shape=jax.ShapeDtypeStruct(flat.shape, BF),
        in_specs=[VMEM] * (1 + n),
        out_specs=VMEM,
        scratch_shapes=[pltpu.VMEM((pairs, cols, lanes), BF), pltpu.VMEM(flat.shape, F32)],
        compiler_params=params(),
        cost_estimate=cost(0, volume.size * 10),
    )(base, *spec)
    return out.reshape(volume.shape)


def solution(mesh):
    placed = (P(None, "depth", None, "gx"), P(), P(), P("depth", None, None))
    return jax.shard_map(
        block, mesh=mesh, in_specs=placed, out_specs=P(None, "depth", None, "gx"), check_vma=False
    )
```

profile of v0, /device:TPU:16, one launch (start us, length us, event | category | flops | bytes accessed | tf_op | source)
XLA Modules:
  0.0 66.2 jit_solution(15219521873190296041)
XLA Ops:
  0.0 0.0 copy-start
  0.0 1.1 %copy-done = bf16[64,24,2,128]{3,2,1,0:T(2,128)(2,1)S(1)} copy-done((bf16[64,24,2,128]{3,2,1,0:T(2,128)(2,1)S(1)}, bf16[64,24,2,128]{3,2,1,0:T(2,128)(2,1)}, u32[]{:S(2)}) %copy-start) | copy-done | bytes 786456
  1.1 0.0 copy-start.4
  1.1 0.9 %copy-done.4 = bf16[8,64,64]{2,1,0:T(8,128)(2,1)S(1)} copy-done((bf16[8,64,64]{2,1,0:T(8,128)(2,1)S(1)}, bf16[8,64,64]{2,1,0:T(8,128)(2,1)}, u32[]{:S(2)}) %copy-start.4) | copy-done | bytes 65560
  2.0 0.8 %shard_map.46 = (bf16[12,128,256]{2,1,0:T(8,128)(2,1)S(1)}, bf16[512,128]{1,0:T(8,128)(2,1)S(1)}, bf16[512,128]{1,0:T(8,128)(2,1)S(1)}, bf16[512,128]{1,0:T(8,12...) custom-call(bf16[3072,128]{1,0:T(8,128)(2,1)S(1)} %bitcast.44, ...), custom_call_target="tpu_custom_call" | custom-call | bytes 2359296 | tf_op jit(solution)/shard_map/pallas_call | solution.py:275
  2.8 0.0 copy-start.2
  2.8 0.0 copy-start.3
  2.9 1.6 %collective-permute-start.4 = (bf16[512,128]{1,0:T(8,128)(2,1)S(1)}, bf16[512,128]{1,0:T(8,128)(2,1)S(1)}, u32[]{:S(2)}, u32[]{:S(2)}) collective-permute-start(bf16[512,128]{1,0:T(8,128)(2,1)S(1)} %get-tuple-element.28), channel_id=1, source_target_pairs={{0,4},{4,0},{8,12},{12,8},{16,20},{20,16},{24,28},{28,24},{1,5},{5... | collective-permute-start | bytes 393224 | tf_op jit(solution)/shard_map/ppermute | solution.py:271
  4.4 1.6 %collective-permute-start.5 = (bf16[512,128]{1,0:T(8,128)(2,1)S(1)}, bf16[512,128]{1,0:T(8,128)(2,1)S(1)}, u32[]{:S(2)}, u32[]{:S(2)}) collective-permute-start(bf16[512,128]{1,0:T(8,128)(2,1)S(1)} %get-tuple-element.29), channel_id=1, source_target_pairs={{0,8},{4,12},{8,0},{12,4},{16,24},{20,28},{24,16},{28,20},{1,9},{5... | collective-permute-start | bytes 393224 | tf_op jit(solution)/shard_map/ppermute | solution.py:271
  6.0 0.4 collective-permute-start.6
  6.4 0.0 collective-permute-start.7
  6.4 1.3 %collective-permute-start = (bf16[12,2,256]{2,1,0:T(2,128)(2,1)S(1)}, bf16[12,2,256]{2,1,0:T(2,128)(2,1)S(1)}, u32[]{:S(2)}, u32[]{:S(2)}) collective-permute-start(bf16[12,2,256]{2,1,0:T(2,128)(2,1)S(1)} %get-tuple-element.45), channel_id=1, source_target_pairs={{1,0},{2,1},{3,2},{5,4},{6,5},{7,6},{9,8},{10,9},{11,10},{13,12},{... | collective-permute-start | bytes 36872 | tf_op jit(solution)/shard_map/ppermute | solution.py:244
  7.8 0.1 fusion.8
  7.8 0.1 add.124
  7.9 0.1 add.127
  8.0 0.1 broadcast_compare_fusion
  8.1 0.1 fusion.9
  8.2 0.1 add_convert_fusion
  8.3 0.1 convert_element_type.24
  8.4 0.0 copy-start.1
  8.4 0.4 multiply_convert_fusion.basis_t
  8.8 0.3 multiply_convert_fusion.1.basis
  9.1 0.4 collective-permute-done.right
  9.5 3.8 %collective-permute-start.8 = (bf16[512,128]{1,0:T(8,128)(2,1)S(1)}, bf16[512,128]{1,0:T(8,128)(2,1)S(1)}, u32[]{:S(2)}, u32[]{:S(2)}) collective-permute-start(bf16[512,128]{1,0:T(8,128)(2,1)S(1)} %get-tuple-element.32), channel_id=1, source_target_pairs={{0,20},{4,16},{8,28},{12,24},{16,4},{20,0},{24,12},{28,8},{1,21},{... | collective-permute-start | bytes 393224 | tf_op jit(solution)/shard_map/ppermute | solution.py:271
  13.4 0.0 collective-permute-done.4.refs_1_
  13.4 0.5 collective-permute-start.9
  13.9 0.0 collective-permute-done.5.refs_2_
  13.9 1.6 %collective-permute-start.10 = (bf16[512,128]{1,0:T(8,128)(2,1)S(1)}, bf16[512,128]{1,0:T(8,128)(2,1)S(1)}, u32[]{:S(2)}, u32[]{:S(2)}) collective-permute-start(bf16[512,128]{1,0:T(8,128)(2,1)S(1)} %get-tuple-element.34), channel_id=1, source_target_pairs={{0,28},{4,24},{8,20},{12,16},{16,12},{20,8},{24,4},{28,0},{1,29},{... | collective-permute-start | bytes 393224 | tf_op jit(solution)/shard_map/ppermute | solution.py:271
  15.5 0.0 collective-permute-done.6.refs_3_
  15.5 3.2 %collective-permute-start.1 = (bf16[12,2,256]{2,1,0:T(2,128)(2,1)S(1)}, bf16[12,2,256]{2,1,0:T(2,128)(2,1)S(1)}, u32[]{:S(2)}, u32[]{:S(2)}) collective-permute-start(bf16[12,2,256]{2,1,0:T(2,128)(2,1)S(1)} %get-tuple-element.46), channel_id=1, source_target_pairs={{0,1},{1,2},{2,3},{4,5},{5,6},{6,7},{8,9},{9,10},{10,11},{12,13},{... | collective-permute-start | bytes 36872 | tf_op jit(solution)/shard_map/ppermute | solution.py:244
  18.8 0.0 collective-permute-done.7.refs_4_
  18.8 5.6 %collective-permute-done.8.refs_5_ = bf16[512,128]{1,0:T(8,128)(2,1)S(1)} collective-permute-done((bf16[512,128]{1,0:T(8,128)(2,1)S(1)}, bf16[512,128]{1,0:T(8,128)(2,1)S(1)}, u32[]{:S(2)}, u32[]{:S(2)}) %collective-permute-start.8) | collective-permute-done | bytes 131104 | tf_op jit(solution)/shard_map/ppermute | solution.py:271
  24.4 4.8 %collective-permute-done.9.refs_6_ = bf16[512,128]{1,0:T(8,128)(2,1)S(1)} collective-permute-done((bf16[512,128]{1,0:T(8,128)(2,1)S(1)}, bf16[512,128]{1,0:T(8,128)(2,1)S(1)}, u32[]{:S(2)}, u32[]{:S(2)}) %collective-permute-start.9) | collective-permute-done | bytes 131104 | tf_op jit(solution)/shard_map/ppermute | solution.py:271
  29.3 3.1 %collective-permute-done.10.refs_7_ = bf16[512,128]{1,0:T(8,128)(2,1)S(1)} collective-permute-done((bf16[512,128]{1,0:T(8,128)(2,1)S(1)}, bf16[512,128]{1,0:T(8,128)(2,1)S(1)}, u32[]{:S(2)}, u32[]{:S(2)}) %collective-permute-start.10) | collective-permute-done | bytes 131104 | tf_op jit(solution)/shard_map/ppermute | solution.py:271
  32.4 0.0 collective-permute-start.11
  32.4 0.0 collective-permute-done.1.left
  32.5 4.0 %collective-permute-start.3 = (bf16[132,256]{1,0:T(8,128)(2,1)S(1)}, bf16[132,256]{1,0:T(8,128)(2,1)S(1)}, u32[]{:S(2)}, u32[]{:S(2)}) collective-permute-start(bf16[132,256]{1,0:T(8,128)(2,1)S(1)} %pad_maximum_fusion.1), channel_id=1, source_target_pairs={{4,0},{8,4},{12,8},{16,12},{20,16},{24,20},{28,24},{5,1},{9,5},{13... | collective-permute-start | bytes 202760 | tf_op jit(solution)/shard_map/ppermute | solution.py:244
  36.5 0.0 collective-permute-done.11.other
  36.5 2.0 %shard_map.49 = (bf16[384,128]{1,0:T(8,128)(2,1)S(1)}, bf16[384,128]{1,0:T(8,128)(2,1)S(1)}, bf16[384,128]{1,0:T(8,128)(2,1)S(1)}, bf16[384,128]{1,0:T(8,128)(2,...) custom-call(bf16[64,192]{1,0:T(8,128)(2,1)S(1)} %multiply_convert_fu, ...), custom_call_target="tpu_custom_call" | custom-call | flops 100663296 | bytes 2359296 | tf_op jit(solution)/shard_map/pallas_call | solution.py:315
  38.5 0.1 collective-permute-start.12
  38.6 0.7 %collective-permute-start.13 = (bf16[384,128]{1,0:T(8,128)(2,1)S(1)}, bf16[384,128]{1,0:T(8,128)(2,1)S(1)}, u32[]{:S(2)}, u32[]{:S(2)}) collective-permute-start(bf16[384,128]{1,0:T(8,128)(2,1)S(1)} %get-tuple-element.37), channel_id=1, source_target_pairs={{0,8},{4,12},{8,0},{12,4},{16,24},{20,28},{24,16},{28,20},{1,9},{5... | collective-permute-start | bytes 294920 | tf_op jit(solution)/shard_map/ppermute | solution.py:271
  39.3 3.9 %collective-permute-start.2 = (bf16[132,256]{1,0:T(8,128)(2,1)S(1)}, bf16[132,256]{1,0:T(8,128)(2,1)S(1)}, u32[]{:S(2)}, u32[]{:S(2)}) collective-permute-start(bf16[132,256]{1,0:T(8,128)(2,1)S(1)} %pad_maximum_fusion), channel_id=1, source_target_pairs={{0,4},{4,8},{8,12},{12,16},{16,20},{20,24},{24,28},{1,5},{5,9},{9,... | collective-permute-start | bytes 202760 | tf_op jit(solution)/shard_map/ppermute | solution.py:244
  43.2 0.0 copy-done.2
  43.2 0.0 copy-done.3
  43.2 0.4 shard_map.47
  43.6 0.3 collective-permute-start.14
  43.9 0.0 collective-permute-done.3.after
  43.9 2.2 %collective-permute-start.15 = (bf16[384,128]{1,0:T(8,128)(2,1)S(1)}, bf16[384,128]{1,0:T(8,128)(2,1)S(1)}, u32[]{:S(2)}, u32[]{:S(2)}) collective-permute-start(bf16[384,128]{1,0:T(8,128)(2,1)S(1)} %get-tuple-element.39), channel_id=1, source_target_pairs={{0,16},{4,20},{8,24},{12,28},{16,0},{20,4},{24,8},{28,12},{1,17},{... | collective-permute-start | bytes 294920 | tf_op jit(solution)/shard_map/ppermute | solution.py:271
  46.1 0.3 collective-permute-done.2.before
  46.4 2.5 %collective-permute-start.16 = (bf16[384,128]{1,0:T(8,128)(2,1)S(1)}, bf16[384,128]{1,0:T(8,128)(2,1)S(1)}, u32[]{:S(2)}, u32[]{:S(2)}) collective-permute-start(bf16[384,128]{1,0:T(8,128)(2,1)S(1)} %get-tuple-element.40), channel_id=1, source_target_pairs={{0,20},{4,16},{8,28},{12,24},{16,4},{20,0},{24,12},{28,8},{1,21},{... | collective-permute-start | bytes 294920 | tf_op jit(solution)/shard_map/ppermute | solution.py:271
  48.9 0.0 collective-permute-done.12.refs_1_
  48.9 2.1 %collective-permute-start.17 = (bf16[384,128]{1,0:T(8,128)(2,1)S(1)}, bf16[384,128]{1,0:T(8,128)(2,1)S(1)}, u32[]{:S(2)}, u32[]{:S(2)}) collective-permute-start(bf16[384,128]{1,0:T(8,128)(2,1)S(1)} %get-tuple-element.41), channel_id=1, source_target_pairs={{0,24},{4,28},{8,16},{12,20},{16,8},{20,12},{24,0},{28,4},{1,25},{... | collective-permute-start | bytes 294920 | tf_op jit(solution)/shard_map/ppermute | solution.py:271
  51.0 0.0 collective-permute-done.13.refs_2_
  51.0 0.0 collective-permute-start.18
  51.0 0.0 copy-done.1
  51.0 3.4 %shard_map.48.base = f32[3072,128]{1,0:T(8,128)S(1)} custom-call(bf16[3072,128]{1,0:T(8,128)(2,1)S(1)} %bitcast.45, bf16[12,128,256]{2,1,0:T(8,128)(2,1)S(1)} %get-tuple-element.24.vt, bf16[132,256]{1,0:T(8,128)(2,1)S(1)} %collective-permute-done.2.before, bf16[132,256]{1,0:T(8,128)(2,1)S(1)} %collective-permute-done.3.after, ...), custom_call_target="tpu_custom_call" | custom-call | flops 2415919104 | bytes 3145728 | tf_op jit(solution)/shard_map/pallas_call | solution.py:330
  54.4 0.0 collective-permute-done.14.refs_3_
  54.4 2.4 %collective-permute-done.15.refs_4_ = bf16[384,128]{1,0:T(8,128)(2,1)S(1)} collective-permute-done((bf16[384,128]{1,0:T(8,128)(2,1)S(1)}, bf16[384,128]{1,0:T(8,128)(2,1)S(1)}, u32[]{:S(2)}, u32[]{:S(2)}) %collective-permute-start.15) | collective-permute-done | bytes 98336 | tf_op jit(solution)/shard_map/ppermute | solution.py:271
  56.8 2.1 %collective-permute-done.16.refs_5_ = bf16[384,128]{1,0:T(8,128)(2,1)S(1)} collective-permute-done((bf16[384,128]{1,0:T(8,128)(2,1)S(1)}, bf16[384,128]{1,0:T(8,128)(2,1)S(1)}, u32[]{:S(2)}, u32[]{:S(2)}) %collective-permute-start.16) | collective-permute-done | bytes 98336 | tf_op jit(solution)/shard_map/ppermute | solution.py:271
  58.9 3.8 %collective-permute-done.17.refs_6_ = bf16[384,128]{1,0:T(8,128)(2,1)S(1)} collective-permute-done((bf16[384,128]{1,0:T(8,128)(2,1)S(1)}, bf16[384,128]{1,0:T(8,128)(2,1)S(1)}, u32[]{:S(2)}, u32[]{:S(2)}) %collective-permute-start.17) | collective-permute-done | bytes 98336 | tf_op jit(solution)/shard_map/ppermute | solution.py:271
  62.7 1.7 %collective-permute-done.18.refs_7_ = bf16[384,128]{1,0:T(8,128)(2,1)S(1)} collective-permute-done((bf16[384,128]{1,0:T(8,128)(2,1)S(1)}, bf16[384,128]{1,0:T(8,128)(2,1)S(1)}, u32[]{:S(2)}, u32[]{:S(2)}) %collective-permute-start.18) | collective-permute-done | bytes 98336 | tf_op jit(solution)/shard_map/ppermute | solution.py:271
  64.4 1.7 %shard_map.50 = bf16[3072,128]{1,0:T(8,128)(2,1)} custom-call(f32[3072,128]{1,0:T(8,128)S(1)} %shard_map.48.base, bf16[384,128]{1,0:T(8,128)(2,1)S(1)} %get-tuple-element.35.refs_0_, bf16[384,128]{1,0:T(8,128)(2,1)S(1)} %collective-permute-done.12.refs_1_, bf16[384,128]{1,0:T(8,128)(2,1)S(1)} %collective-permute-done.13.refs_2_, ...), custom_call_target="tpu_custom_call" | custom-call | bytes 3932160 | tf_op jit(solution)/shard_map/pallas_call | solution.py:343
  (17 shorter events, 0.1 us)
Async XLA Ops:
  0.0 1.1 %copy-start = (bf16[64,24,2,128]{3,2,1,0:T(2,128)(2,1)S(1)}, bf16[64,24,2,128]{3,2,1,0:T(2,128)(2,1)}, u32[]{:S(2)}) copy-start(bf16[64,24,2,128]{3,2,1,0:T(2,128)(2,1)} %param.4) | copy-start | bytes 2359300
  1.1 0.9 %copy-start.4 = (bf16[8,64,64]{2,1,0:T(8,128)(2,1)S(1)}, bf16[8,64,64]{2,1,0:T(8,128)(2,1)}, u32[]{:S(2)}) copy-start(bf16[8,64,64]{2,1,0:T(8,128)(2,1)} %weights.1) | copy-start | bytes 196612
  2.8 40.3 %copy-start.2 = (bf16[3,3,3,64,64]{4,3,2,1,0:T(8,128)(2,1)S(1)}, bf16[3,3,3,64,64]{4,3,2,1,0:T(8,128)(2,1)}, u32[]{:S(2)}) copy-start(bf16[3,3,3,64,64]{4,3,2,1,0:T(8,128)(2,1)} %first.1) | copy-start | bytes 663556
  2.8 40.3 %copy-start.3 = (bf16[3,3,3,64,64]{4,3,2,1,0:T(8,128)(2,1)S(1)}, bf16[3,3,3,64,64]{4,3,2,1,0:T(8,128)(2,1)}, u32[]{:S(2)}) copy-start(bf16[3,3,3,64,64]{4,3,2,1,0:T(8,128)(2,1)} %second.1) | copy-start | bytes 663556
  2.9 10.5 %collective-permute-start.4 = (bf16[512,128]{1,0:T(8,128)(2,1)S(1)}, bf16[512,128]{1,0:T(8,128)(2,1)S(1)}, u32[]{:S(2)}, u32[]{:S(2)}) collective-permute-start(bf16[512,128]{1,0:T(8,128)(2,1)S(1)} %get-tuple-element.28), channel_id=1, source_target_pairs={{0,4},{4,0},{8,12},{12,8},{16,20},{20,16},{24,28},{28,24},{1,5},{5... | collective-permute-start | bytes 393224 | tf_op jit(solution)/shard_map/ppermute | solution.py:271
  4.4 9.5 %collective-permute-start.5 = (bf16[512,128]{1,0:T(8,128)(2,1)S(1)}, bf16[512,128]{1,0:T(8,128)(2,1)S(1)}, u32[]{:S(2)}, u32[]{:S(2)}) collective-permute-start(bf16[512,128]{1,0:T(8,128)(2,1)S(1)} %get-tuple-element.29), channel_id=1, source_target_pairs={{0,8},{4,12},{8,0},{12,4},{16,24},{20,28},{24,16},{28,20},{1,9},{5... | collective-permute-start | bytes 393224 | tf_op jit(solution)/shard_map/ppermute | solution.py:271
  6.0 9.5 %collective-permute-start.6 = (bf16[512,128]{1,0:T(8,128)(2,1)S(1)}, bf16[512,128]{1,0:T(8,128)(2,1)S(1)}, u32[]{:S(2)}, u32[]{:S(2)}) collective-permute-start(bf16[512,128]{1,0:T(8,128)(2,1)S(1)} %get-tuple-element.30), channel_id=1, source_target_pairs={{0,12},{4,8},{8,4},{12,0},{16,28},{20,24},{24,20},{28,16},{1,13},{... | collective-permute-start | bytes 393224 | tf_op jit(solution)/shard_map/ppermute | solution.py:271
  6.4 12.3 %collective-permute-start.7 = (bf16[512,128]{1,0:T(8,128)(2,1)S(1)}, bf16[512,128]{1,0:T(8,128)(2,1)S(1)}, u32[]{:S(2)}, u32[]{:S(2)}) collective-permute-start(bf16[512,128]{1,0:T(8,128)(2,1)S(1)} %get-tuple-element.31), channel_id=1, source_target_pairs={{0,16},{4,20},{8,24},{12,28},{16,0},{20,4},{24,8},{28,12},{1,17},{... | collective-permute-start | bytes 393224 | tf_op jit(solution)/shard_map/ppermute | solution.py:271
  6.4 3.1 %collective-permute-start = (bf16[12,2,256]{2,1,0:T(2,128)(2,1)S(1)}, bf16[12,2,256]{2,1,0:T(2,128)(2,1)S(1)}, u32[]{:S(2)}, u32[]{:S(2)}) collective-permute-start(bf16[12,2,256]{2,1,0:T(2,128)(2,1)S(1)} %get-tuple-element.45), channel_id=1, source_target_pairs={{1,0},{2,1},{3,2},{5,4},{6,5},{7,6},{9,8},{10,9},{11,10},{13,12},{... | collective-permute-start | bytes 36872 | tf_op jit(solution)/shard_map/ppermute | solution.py:244
  8.4 42.6 %copy-start.1 = (bf16[64,24,2,128]{3,2,1,0:T(2,128)(2,1)S(1)}, bf16[64,24,2,128]{3,2,1,0:T(2,128)(2,1)}, u32[]{:S(2)}) copy-start(bf16[64,24,2,128]{3,2,1,0:T(2,128)(2,1)} %param.4) | copy-start | bytes 2359300
  9.5 14.9 %collective-permute-start.8 = (bf16[512,128]{1,0:T(8,128)(2,1)S(1)}, bf16[512,128]{1,0:T(8,128)(2,1)S(1)}, u32[]{:S(2)}, u32[]{:S(2)}) collective-permute-start(bf16[512,128]{1,0:T(8,128)(2,1)S(1)} %get-tuple-element.32), channel_id=1, source_target_pairs={{0,20},{4,16},{8,28},{12,24},{16,4},{20,0},{24,12},{28,8},{1,21},{... | collective-permute-start | bytes 393224 | tf_op jit(solution)/shard_map/ppermute | solution.py:271
  13.4 15.9 %collective-permute-start.9 = (bf16[512,128]{1,0:T(8,128)(2,1)S(1)}, bf16[512,128]{1,0:T(8,128)(2,1)S(1)}, u32[]{:S(2)}, u32[]{:S(2)}) collective-permute-start(bf16[512,128]{1,0:T(8,128)(2,1)S(1)} %get-tuple-element.33), channel_id=1, source_target_pairs={{0,24},{4,28},{8,16},{12,20},{16,8},{20,12},{24,0},{28,4},{1,25},{... | collective-permute-start | bytes 393224 | tf_op jit(solution)/shard_map/ppermute | solution.py:271
  13.9 18.5 %collective-permute-start.10 = (bf16[512,128]{1,0:T(8,128)(2,1)S(1)}, bf16[512,128]{1,0:T(8,128)(2,1)S(1)}, u32[]{:S(2)}, u32[]{:S(2)}) collective-permute-start(bf16[512,128]{1,0:T(8,128)(2,1)S(1)} %get-tuple-element.34), channel_id=1, source_target_pairs={{0,28},{4,24},{8,20},{12,16},{16,12},{20,8},{24,4},{28,0},{1,29},{... | collective-permute-start | bytes 393224 | tf_op jit(solution)/shard_map/ppermute | solution.py:271
  15.5 16.9 %collective-permute-start.1 = (bf16[12,2,256]{2,1,0:T(2,128)(2,1)S(1)}, bf16[12,2,256]{2,1,0:T(2,128)(2,1)S(1)}, u32[]{:S(2)}, u32[]{:S(2)}) collective-permute-start(bf16[12,2,256]{2,1,0:T(2,128)(2,1)S(1)} %get-tuple-element.46), channel_id=1, source_target_pairs={{0,1},{1,2},{2,3},{4,5},{5,6},{6,7},{8,9},{9,10},{10,11},{12,13},{... | collective-permute-start | bytes 36872 | tf_op jit(solution)/shard_map/ppermute | solution.py:244
  32.4 4.0 %collective-permute-start.11 = (bf16[8,128,128]{2,1,0:T(8,128)(2,1)S(1)}, bf16[8,128,128]{2,1,0:T(8,128)(2,1)S(1)}, u32[]{:S(2)}, u32[]{:S(2)}) collective-permute-start(bf16[8,128,128]{2,1,0:T(8,128)(2,1)S(1)} %fusion), channel_id=1, source_target_pairs={{0,1},{1,0},{2,3},{3,2},{4,5},{5,4},{6,7},{7,6},{8,9},{9,8},{10,11... | collective-permute-start | bytes 786440 | tf_op jit(solution)/shard_map/ppermute | solution.py:304
  32.5 11.4 %collective-permute-start.3 = (bf16[132,256]{1,0:T(8,128)(2,1)S(1)}, bf16[132,256]{1,0:T(8,128)(2,1)S(1)}, u32[]{:S(2)}, u32[]{:S(2)}) collective-permute-start(bf16[132,256]{1,0:T(8,128)(2,1)S(1)} %pad_maximum_fusion.1), channel_id=1, source_target_pairs={{4,0},{8,4},{12,8},{16,12},{20,16},{24,20},{28,24},{5,1},{9,5},{13... | collective-permute-start | bytes 202760 | tf_op jit(solution)/shard_map/ppermute | solution.py:244
  38.5 10.3 %collective-permute-start.12 = (bf16[384,128]{1,0:T(8,128)(2,1)S(1)}, bf16[384,128]{1,0:T(8,128)(2,1)S(1)}, u32[]{:S(2)}, u32[]{:S(2)}) collective-permute-start(bf16[384,128]{1,0:T(8,128)(2,1)S(1)} %get-tuple-element.36), channel_id=1, source_target_pairs={{0,4},{4,0},{8,12},{12,8},{16,20},{20,16},{24,28},{28,24},{1,5},{5... | collective-permute-start | bytes 294920 | tf_op jit(solution)/shard_map/ppermute | solution.py:271
  38.6 12.4 %collective-permute-start.13 = (bf16[384,128]{1,0:T(8,128)(2,1)S(1)}, bf16[384,128]{1,0:T(8,128)(2,1)S(1)}, u32[]{:S(2)}, u32[]{:S(2)}) collective-permute-start(bf16[384,128]{1,0:T(8,128)(2,1)S(1)} %get-tuple-element.37), channel_id=1, source_target_pairs={{0,8},{4,12},{8,0},{12,4},{16,24},{20,28},{24,16},{28,20},{1,9},{5... | collective-permute-start | bytes 294920 | tf_op jit(solution)/shard_map/ppermute | solution.py:271
  39.3 7.1 %collective-permute-start.2 = (bf16[132,256]{1,0:T(8,128)(2,1)S(1)}, bf16[132,256]{1,0:T(8,128)(2,1)S(1)}, u32[]{:S(2)}, u32[]{:S(2)}) collective-permute-start(bf16[132,256]{1,0:T(8,128)(2,1)S(1)} %pad_maximum_fusion), channel_id=1, source_target_pairs={{0,4},{4,8},{8,12},{12,16},{16,20},{20,24},{24,28},{1,5},{5,9},{9,... | collective-permute-start | bytes 202760 | tf_op jit(solution)/shard_map/ppermute | solution.py:244
  43.6 10.8 %collective-permute-start.14 = (bf16[384,128]{1,0:T(8,128)(2,1)S(1)}, bf16[384,128]{1,0:T(8,128)(2,1)S(1)}, u32[]{:S(2)}, u32[]{:S(2)}) collective-permute-start(bf16[384,128]{1,0:T(8,128)(2,1)S(1)} %get-tuple-element.38), channel_id=1, source_target_pairs={{0,12},{4,8},{8,4},{12,0},{16,28},{20,24},{24,20},{28,16},{1,13},{... | collective-permute-start | bytes 294920 | tf_op jit(solution)/shard_map/ppermute | solution.py:271
  43.9 12.9 %collective-permute-start.15 = (bf16[384,128]{1,0:T(8,128)(2,1)S(1)}, bf16[384,128]{1,0:T(8,128)(2,1)S(1)}, u32[]{:S(2)}, u32[]{:S(2)}) collective-permute-start(bf16[384,128]{1,0:T(8,128)(2,1)S(1)} %get-tuple-element.39), channel_id=1, source_target_pairs={{0,16},{4,20},{8,24},{12,28},{16,0},{20,4},{24,8},{28,12},{1,17},{... | collective-permute-start | bytes 294920 | tf_op jit(solution)/shard_map/ppermute | solution.py:271
  46.4 12.5 %collective-permute-start.16 = (bf16[384,128]{1,0:T(8,128)(2,1)S(1)}, bf16[384,128]{1,0:T(8,128)(2,1)S(1)}, u32[]{:S(2)}, u32[]{:S(2)}) collective-permute-start(bf16[384,128]{1,0:T(8,128)(2,1)S(1)} %get-tuple-element.40), channel_id=1, source_target_pairs={{0,20},{4,16},{8,28},{12,24},{16,4},{20,0},{24,12},{28,8},{1,21},{... | collective-permute-start | bytes 294920 | tf_op jit(solution)/shard_map/ppermute | solution.py:271
  48.9 13.8 %collective-permute-start.17 = (bf16[384,128]{1,0:T(8,128)(2,1)S(1)}, bf16[384,128]{1,0:T(8,128)(2,1)S(1)}, u32[]{:S(2)}, u32[]{:S(2)}) collective-permute-start(bf16[384,128]{1,0:T(8,128)(2,1)S(1)} %get-tuple-element.41), channel_id=1, source_target_pairs={{0,24},{4,28},{8,16},{12,20},{16,8},{20,12},{24,0},{28,4},{1,25},{... | collective-permute-start | bytes 294920 | tf_op jit(solution)/shard_map/ppermute | solution.py:271
  51.0 13.4 %collective-permute-start.18 = (bf16[384,128]{1,0:T(8,128)(2,1)S(1)}, bf16[384,128]{1,0:T(8,128)(2,1)S(1)}, u32[]{:S(2)}, u32[]{:S(2)}) collective-permute-start(bf16[384,128]{1,0:T(8,128)(2,1)S(1)} %get-tuple-element.42), channel_id=1, source_target_pairs={{0,28},{4,24},{8,20},{12,16},{16,12},{20,8},{24,4},{28,0},{1,29},{... | collective-permute-start | bytes 294920 | tf_op jit(solution)/shard_map/ppermute | solution.py:271
where the time goes:
time: 66.4 us; the launch traced here: 66.2 us
  starting transfers between devices  29.7 us (45%)
  waiting for transfers between devices  24.4 us (37%)
  Pallas kernels  8.31 us (13%)
  local copies, waits for them, and re-layouts  2.42 us (4%)
  other arithmetic  1.09 us (2%)
    ppermute x14, waiting for transfers between devices, send(): return lax.ppermute(value, 'depth', table)  23.7 us
    ppermute x14, starting transfers between devices, send(): return lax.ppermute(value, 'depth', table)  17.4 us
    ppermute x4, starting transfers between devices, shift_line(): return lax.ppermute(value, axis, pairs)  12.3 us
    pallas_call x1, Pallas kernels, block(): pl.pallas_call(functools.partial(conv_kernel, ngx, n), out_shape=jax.Shap...  3.36 us
    unnamed x17, local copies, waits for them, and re-layouts  2.12 us
    pallas_call x1, Pallas kernels, block(): pl.pallas_call(spectral_kernel, out_shape=[jax.ShapeDtypeStruct((2 * per,...  2.05 us
    pallas_call x1, Pallas kernels, block(): pl.pallas_call(join_kernel, out_shape=jax.ShapeDtypeStruct(flat.shape, BF...  1.75 us
  transfers between devices with their start and end apart: 19, of which 9 were waited for; matrix products, arithmetic and copies ran while one was open for 2% of the time, Pallas kernels for 9%

commit v1 on v0

v1 whole, which is shorter than its diff:
```python
import functools
import math

import jax
import jax.numpy as jnp
from jax import lax
from jax.experimental import pallas as pl
from jax.experimental.pallas import tpu as pltpu
from jax.sharding import PartitionSpec as P


MODES = 32
BF = jnp.bfloat16
F32 = jnp.float32
VMEM = pl.BlockSpec(memory_space=pltpu.VMEM)
HBM = pl.BlockSpec(memory_space=pltpu.HBM)


def mode_basis(mode_index, depth_pos, total_z):
    frequency = jnp.where(mode_index < MODES, mode_index, mode_index - MODES + 1).astype(F32)
    odd_steps = (2 * depth_pos + 1).astype(F32)
    angles = frequency * odd_steps * (math.pi / (2.0 * total_z))
    values = jnp.where(mode_index < MODES, jnp.cos(angles), jnp.sin(angles))
    return values * math.sqrt(2.0 / total_z)


def cost(flops, nbytes, trans=0):
    return pl.CostEstimate(flops=flops, bytes_accessed=nbytes, transcendentals=trans)


def in_hbm(value):
    return pltpu.with_memory_space_constraint(value, pltpu.HBM)


def params():
    return pltpu.CompilerParams(vmem_limit_bytes=20 * 1024 * 1024)


def target(k):
    me = lax.axis_index("depth")
    return me ^ k


def split_kernel(slab, flat, weights, vt, odd, *refs):
    *chunks, held, modes, wide, sem = refs
    pairs, cols, lanes = vt.shape
    n = len(chunks)
    part = cols // n
    half = lanes // 2
    own = weights.shape[0] // 2
    ch = weights.shape[2]
    stride = flat.shape[0] // ch
    ny = stride // slab
    core = lax.axis_index("gx") % 2
    upper = lax.axis_index("depth") % 2
    block = flat.shape[0] // 4
    loads = [
        pltpu.make_async_copy(
            flat.at[pl.ds(i * block, block), :], held.at[pl.ds(i * block, block), :], sem.at[i]
        )
        for i in range(4)
    ]
    loads.append(pltpu.make_async_copy(weights.at[pl.ds(core * own, own)], modes, sem.at[4]))
    for load in loads:
        load.start()
    for i in range(4):
        loads[i].wait()
        wide[pl.ds(i * block, block), :] = held[pl.ds(i * block, block), :].astype(F32)
    for q in range(pairs):
        rows = [wide[pl.ds(2 * q * ny + j, ch, stride=stride), :] for j in range(2 * ny)]
        vt[q] = jnp.concatenate(rows, axis=0).astype(BF).T
    body = 2 * pairs * part
    loads[4].wait()
    for k in range(n):
        start = pl.multiple_of(target(k) * part, part)
        for q in range(pairs):
            for par in range(2):
                chunks[k][pl.ds((par * pairs + q) * part, part), :] = vt[
                    q, pl.ds(start, part), pl.ds(par * half, half)
                ]
        if k <= n // 2:
            for j in range(own // 2):
                chunks[k][pl.ds(body + j * ch, ch), :] = jnp.concatenate(
                    [modes[2 * j], modes[2 * j + 1]], axis=1
                )
    tail = body + own // 2 * ch
    for par in range(2):
        lane = pl.ds(par * half, half)
        chunks[1][pl.ds(tail + par * cols, cols), :] = vt[(1 - upper) * (pairs - 1), :, lane]
        odd[pl.ds(par * cols, cols), :] = vt[upper * (pairs - 1), :, lane]


def ends_of(near, odd, cols):
    upper = lax.axis_index("depth") % 2 == 1
    tail = near.shape[0] - 2 * cols
    one = jnp.concatenate([near[pl.ds(tail, cols), :], near[pl.ds(tail + cols, cols), :]], axis=1)
    two = jnp.concatenate([odd[pl.ds(0, cols), :], odd[pl.ds(cols, cols), :]], axis=1)
    one, two = one.astype(F32), two.astype(F32)
    return jnp.where(upper, one, two), jnp.where(upper, two, one)


def strips_kernel(vt, near, odd, even_out, odd_out):
    pairs, cols, _ = vt.shape
    before, after = ends_of(near, odd, cols)
    mids = [before] + [vt[q].astype(F32) for q in range(pairs)] + [after]
    head = jnp.concatenate([m[:2] for m in mids], axis=0)
    tail = jnp.concatenate([m[cols - 2 :] for m in mids], axis=0)
    upper = lax.axis_index("gx") % 2 == 1
    even_out[...] = jnp.where(upper, head, tail).astype(BF)
    odd_out[...] = jnp.where(upper, tail, head).astype(BF)


def basis_into(n, slab, out, out_t):
    shape = out.shape
    own = shape[0] // (2 * n)
    pairs = slab // 2
    core = lax.axis_index("gx") % 2
    row = lax.broadcasted_iota(jnp.int32, shape, 0)
    col = lax.broadcasted_iota(jnp.int32, shape, 1)
    mode_index = jnp.zeros(shape, jnp.int32)
    depth_pos = jnp.zeros(shape, jnp.int32)
    for side in range(2):
        for k in range(n):
            at = (side * n + k) * own
            first = target(k) * (2 * own) + (core if side == 0 else 1 - core) * own
            mode_index = jnp.where(row >= at, first + row - at, mode_index)
            at = (side * n + k) * pairs
            first = target(k) * slab + side
            depth_pos = jnp.where(col >= at, first + 2 * (col - at), depth_pos)
    value = mode_basis(mode_index, depth_pos, slab * n)
    out[...] = value.astype(BF)
    out_t[...] = value.T.astype(BF)


def prepare_kernel(n, slab, first, second, basis, basis_t, out_first, out_second, held, sem):
    ch = first.shape[3]
    loads = [
        pltpu.make_async_copy(src, held.at[i], sem.at[i]) for i, src in enumerate((first, second))
    ]
    for load in loads:
        load.start()
    basis_into(n, slab, basis, basis_t)
    for i, dst in ((0, out_first), (1, out_second)):
        loads[i].wait()
        src = held.at[i]
        for e in range(3):
            block = {}
            for a in range(3):
                for yi in range(2):
                    both = jnp.concatenate([src[a, yi + 1, e], src[a, yi, e]], axis=0)
                    block[a, yi] = both.astype(F32).T.astype(BF)
            for h in range(2):
                for pi in range(2):
                    for po in range(2):
                        a = 2 * h + pi - po
                        for yi in range(2):
                            value = block[a, yi] if 0 <= a <= 2 else jnp.zeros((ch, 2 * ch), BF)
                            dst[
                                e * 2 + h,
                                pl.ds((pi * 2 + yi) * ch, ch),
                                pl.ds(po * 2 * ch, 2 * ch),
                            ] = value


def shifted(dst, index, rows, value):
    n = value.shape[0]
    wide = value.astype(F32)
    dst[1, pl.ds(index * rows, rows), :] = value
    dst[0, pl.ds(index * rows, rows), :] = pltpu.roll(wide, 1, 0).astype(BF)
    dst[2, pl.ds(index * rows, rows), :] = pltpu.roll(wide, n - 1, 0).astype(BF)


def conv_kernel(ngx, n, flat, vt, near, odd, even_edge, odd_edge, w1, w2, out, ext, hid):
    pairs, cols, lanes = vt.shape
    rows = cols + 16
    ch = lanes // 4
    me = lax.axis_index("depth")
    gx = lax.axis_index("gx")
    fill = jnp.zeros((rows - cols - 4, lanes), F32)
    before, after = ends_of(near, odd, cols)
    upper = gx % 2 == 1
    even_side, odd_side = even_edge[...].astype(F32), odd_edge[...].astype(F32)
    left = jnp.where(upper, even_side, odd_side)
    right = jnp.where(upper, odd_side, even_side)
    for q in range(pairs + 2):
        mid = before if q == 0 else after if q == pairs + 1 else vt[q - 1].astype(F32)
        ring = jnp.concatenate(
            [mid, right[2 * q : 2 * q + 2], fill, left[2 * q : 2 * q + 2]], axis=0
        ).astype(BF)
        shifted(ext, q, rows, ring)
    at = lax.broadcasted_iota(jnp.int32, (rows, lanes), 0)
    lane = lax.broadcasted_iota(jnp.int32, (rows, lanes), 1)
    inside = jnp.logical_and(
        jnp.logical_or(at != rows - 1, gx > 0), jnp.logical_or(at != cols, gx < ngx - 1)
    )
    for p in range(pairs + 1):
        acc = jnp.zeros((rows, lanes), F32)
        for e in range(3):
            for h in range(2):
                acc += jnp.dot(
                    ext[e, pl.ds((p + h) * rows, rows), :],
                    w1[e * 2 + h],
                    preferred_element_type=F32,
                )
        keep = inside
        if p == 0:
            keep = jnp.logical_and(keep, jnp.logical_or(lane >= lanes // 2, me > 0))
        if p == pairs:
            keep = jnp.logical_and(keep, jnp.logical_or(lane < lanes // 2, me < n - 1))
        value = jnp.where(keep, jax.nn.gelu(acc), 0.0).astype(BF)
        shifted(hid, p, rows, value)
    for p in range(pairs):
        acc = jnp.zeros((cols, lanes), F32)
        for e in range(3):
            for h in range(2):
                acc += jnp.dot(
                    hid[e, pl.ds((p + h) * rows, cols), :],
                    w2[e * 2 + h],
                    preferred_element_type=F32,
                )
        turned = acc.T
        for j in range(4):
            out[p // 2, pl.ds(4 * (p % 2) + j, ch, stride=8), :] = turned[j * ch : (j + 1) * ch]
        if p % 2 == 1:
            own = flat[:, pl.ds(8 * (p // 2), 8), :].astype(F32)
            out[p // 2] += own.reshape(8 * ch, cols)


def gather_kernel(body, *refs):
    *parts, out = refs
    n, rows, _ = out.shape
    for k in range(n):
        out[k] = parts[k][pl.ds(body if k <= n // 2 else 0, rows), :]


def coef_kernel(part, basis, *refs):
    *chunks, coef, field = refs
    n = len(chunks)
    modes = basis.shape[0]
    steps = basis.shape[1] // 2
    per = steps * part // n
    for k in range(n):
        for par in range(2):
            field[par, pl.ds(k * per, per), :] = chunks[k][pl.ds(par * per, per), :].astype(F32)
    for x in range(part):
        piece = jnp.concatenate(
            [field[par, pl.ds(x, steps, stride=part), :].astype(BF) for par in range(2)], axis=0
        )
        coef[pl.ds(x, modes, stride=part), :] = jnp.dot(
            basis[...], piece, preferred_element_type=F32
        )


def spectral_kernel(part, basis_t, coef, mine, other, *refs):
    n = mine.shape[0]
    outs = refs[:n]
    field, mix = refs[n:]
    modes = basis_t.shape[1]
    steps = basis_t.shape[0] // 2
    per = steps * part // n
    wide = mine.shape[2]
    ch = wide // 2
    low = lax.broadcasted_iota(jnp.int32, (part, wide), 1) < ch
    at = 0
    for side in range(2):
        for k in range(n):
            for j in range(mine.shape[1] // ch):
                w = (mine, other)[side][k, pl.ds(j * ch, ch), :]
                c0 = coef[pl.ds(at * part, part), :]
                c1 = coef[pl.ds((at + 1) * part, part), :]
                lhs = jnp.concatenate(
                    [
                        jnp.where(low, c0, 0.0),
                        jnp.where(low, pltpu.roll(c0, ch, 1), 0.0),
                        jnp.where(low, 0.0, pltpu.roll(c1, ch, 1)),
                        jnp.where(low, 0.0, c1),
                    ],
                    axis=0,
                ).astype(BF)
                r = lax.dot_general(
                    lhs, w, (((1,), (1,)), ((), ())), preferred_element_type=F32
                )
                for t in range(2):
                    mix[pl.ds((at + t) * part, part), :] = jnp.concatenate(
                        [
                            r[2 * t * part : (2 * t + 1) * part],
                            r[(2 * t + 1) * part : (2 * t + 2) * part],
                        ],
                        axis=1,
                    )
                at += 2
    for x in range(part):
        value = jnp.dot(
            basis_t[...],
            mix[pl.ds(x, modes, stride=part), :].astype(BF),
            preferred_element_type=F32,
        )
        for par in range(2):
            field[par, pl.ds(x, steps, stride=part), :] = value[par * steps : (par + 1) * steps]
    for k in range(n):
        for par in range(2):
            outs[k][pl.ds(par * per, per), :] = field[par, pl.ds(k * per, per), :].astype(BF)


def join_kernel(base, *refs):
    *chunks, out, total, wide, done, sem = refs
    pairs, cols, lanes = total.shape
    n = len(chunks)
    part = cols // n
    half = lanes // 2
    ch = lanes // 4
    for k in range(n):
        start = pl.multiple_of(target(k) * part, part)
        for q in range(pairs):
            for par in range(2):
                total[q, pl.ds(start, part), pl.ds(par * half, half)] = chunks[k][
                    pl.ds((par * pairs + q) * part, part), :
                ]
    stores = []
    for g in range(pairs // 2):
        for i in range(2):
            turned = total[2 * g + i].T.astype(F32)
            for j in range(4):
                wide[g, pl.ds(4 * i + j, ch, stride=8), :] = turned[j * ch : (j + 1) * ch]
        done[g] = (base[g] + wide[g]).reshape(ch, 8, cols).astype(BF)
        stores.append(
            pltpu.make_async_copy(done.at[g], out.at[:, pl.ds(8 * g, 8), :], sem.at[g])
        )
        stores[g].start()
    for store in stores:
        store.wait()


def swap(value, axis, k):
    count = lax.axis_size(axis)
    return lax.ppermute(value, axis, [(i, i ^ k) for i in range(count) if i ^ k < count])


def swap_odd(value, axis):
    pairs = []
    for i in range(1, lax.axis_size(axis) - 1, 2):
        pairs += [(i, i + 1), (i + 1, i)]
    return lax.ppermute(value, axis, pairs)


def block(volume, conv_first, conv_second, mode_weights):
    ch, slab, ny, cols = volume.shape
    n = lax.axis_size("depth")
    ngx = lax.axis_size("gx")
    assert n & (n - 1) == 0 and n > 2 and ngx % 2 == 0
    pairs = slab // 2
    lanes = 2 * ny * ch
    half = lanes // 2
    part = cols // n
    per = pairs * part
    modes = mode_weights.shape[0] * n
    wrows = mode_weights.shape[0] // 4 * ch
    total_z = slab * n

    flat = volume.reshape(ch * slab * ny, cols)
    sizes = [
        2 * per + (wrows if k <= n // 2 else 0) + (2 * cols if k == 1 else 0) for k in range(n)
    ]
    vt, odd, *chunks = pl.pallas_call(
        functools.partial(split_kernel, slab),
        out_shape=[
            jax.ShapeDtypeStruct((pairs, cols, lanes), BF),
            jax.ShapeDtypeStruct((2 * cols, half), BF),
        ]
        + [jax.ShapeDtypeStruct((size, half), BF) for size in sizes],
        in_specs=[HBM, HBM],
        out_specs=[VMEM] * (n + 2),
        scratch_shapes=[
            pltpu.VMEM(flat.shape, BF),
            pltpu.VMEM((mode_weights.shape[0] // 2,) + mode_weights.shape[1:], BF),
            pltpu.VMEM(flat.shape, F32),
            pltpu.SemaphoreType.DMA((5,)),
        ],
        compiler_params=params(),
        cost_estimate=cost(0, 3 * volume.size * 2),
    )(in_hbm(flat), in_hbm(mode_weights))
    got = [chunks[0]] + [swap(chunks[k], "depth", k) for k in range(1, n)]
    odd = swap_odd(odd, "depth")

    body = slice(2 * per, 2 * per + wrows)
    far = got[n // 2][body]
    passed = [swap(far, "depth", k) for k in range(1, n // 2)]
    mine = pl.pallas_call(
        functools.partial(gather_kernel, 2 * per),
        out_shape=jax.ShapeDtypeStruct((n, wrows, half), BF),
        in_specs=[VMEM] * n,
        out_specs=VMEM,
        compiler_params=params(),
        cost_estimate=cost(0, n * wrows * half * 4),
    )(*got[: n // 2 + 1], *passed)
    other = swap(mine, "gx", 1)

    basis, basis_t, w1, w2 = pl.pallas_call(
        functools.partial(prepare_kernel, n, slab),
        out_shape=[
            jax.ShapeDtypeStruct((modes, total_z), BF),
            jax.ShapeDtypeStruct((total_z, modes), BF),
        ]
        + [jax.ShapeDtypeStruct((6, lanes, lanes), BF)] * 2,
        in_specs=[HBM, HBM],
        out_specs=[VMEM] * 4,
        scratch_shapes=[
            pltpu.VMEM((2,) + conv_first.shape, BF),
            pltpu.SemaphoreType.DMA((2,)),
        ],
        compiler_params=params(),
        cost_estimate=cost(0, 4 * conv_first.size * 2 * 4),
    )(in_hbm(conv_first), in_hbm(conv_second))
    even_edge, odd_edge = pl.pallas_call(
        strips_kernel,
        out_shape=[jax.ShapeDtypeStruct((2 * (pairs + 2), lanes), BF)] * 2,
        in_specs=[VMEM] * 3,
        out_specs=[VMEM] * 2,
        compiler_params=params(),
        cost_estimate=cost(0, 8 * pairs * lanes * 4),
    )(vt, got[1], odd)
    even_edge = swap(even_edge, "gx", 1)
    odd_edge = swap_odd(odd_edge, "gx")

    coef = pl.pallas_call(
        functools.partial(coef_kernel, part),
        out_shape=jax.ShapeDtypeStruct((modes * part, half), F32),
        in_specs=[VMEM] * (1 + n),
        out_specs=VMEM,
        scratch_shapes=[pltpu.VMEM((2, n * per, half), F32)],
        compiler_params=params(),
        cost_estimate=cost(2 * modes * total_z * part * half, 2 * volume.size * 2),
    )(basis, *got)
    outs = pl.pallas_call(
        functools.partial(spectral_kernel, part),
        out_shape=[jax.ShapeDtypeStruct((2 * per, half), BF)] * n,
        in_specs=[VMEM] * 4,
        out_specs=[VMEM] * n,
        scratch_shapes=[pltpu.VMEM((2, n * per, half), F32), pltpu.VMEM((modes * part, half), F32)],
        compiler_params=params(),
        cost_estimate=cost(4 * modes * total_z * part * half, 2 * volume.size * 2),
    )(basis_t, coef, mine, other)
    spec = [outs[0]] + [swap(outs[k], "depth", k) for k in range(1, n)]

    base = pl.pallas_call(
        functools.partial(conv_kernel, ngx, n),
        out_shape=jax.ShapeDtypeStruct((pairs // 2, 8 * ch, cols), F32),
        in_specs=[VMEM] * 8,
        out_specs=VMEM,
        scratch_shapes=[
            pltpu.VMEM((3, (pairs + 2) * (cols + 16), lanes), BF),
            pltpu.VMEM((3, (pairs + 1) * (cols + 16), lanes), BF),
        ],
        compiler_params=params(),
        cost_estimate=cost(4 * 6 * pairs * cols * lanes * lanes, volume.size * 8),
    )(flat.reshape(ch, slab * ny, cols), vt, got[1], odd, even_edge, odd_edge, w1, w2)

    out = pl.pallas_call(
        join_kernel,
        out_shape=jax.ShapeDtypeStruct((ch, slab * ny, cols), BF),
        in_specs=[VMEM] * (1 + n),
        out_specs=HBM,
        scratch_shapes=[
            pltpu.VMEM((pairs, cols, lanes), BF),
            pltpu.VMEM((pairs // 2, 8 * ch, cols), F32),
            pltpu.VMEM((pairs // 2, ch, 8, cols), BF),
            pltpu.SemaphoreType.DMA((pairs // 2,)),
        ],
        compiler_params=params(),
        cost_estimate=cost(0, volume.size * 10),
    )(base, *spec)
    return out.reshape(volume.shape)


def solution(mesh):
    placed = (P(None, "depth", None, "gx"), P(), P(), P("depth", None, None))
    return jax.shard_map(
        block, mesh=mesh, in_specs=placed, out_specs=P(None, "depth", None, "gx"), check_vma=False
    )
```

time: 66.4 us -> 71.5 us (1.077)
  the two profiles are of different devices: /device:TPU:16 before, /device:TPU:17 now
where the time goes in v1:
time: 71.5 us; the launch traced here: 71.3 us
  waiting for transfers between devices  32.1 us (45%)
  starting transfers between devices  29 us (41%)
  Pallas kernels  10.2 us (14%)
    ppermute x19, waiting for transfers between devices, swap(): lax.ppermute(value, axis, [(i, i ^ k) for i in range(count) if i ^ k < co...  28.4 us
    ppermute x19, starting transfers between devices, swap(): lax.ppermute(value, axis, [(i, i ^ k) for i in range(count) if i ^ k < co...  23.2 us
    ppermute x2, starting transfers between devices, swap_odd(): return lax.ppermute(value, axis, pairs)  5.78 us
    ppermute x2, waiting for transfers between devices, swap_odd(): return lax.ppermute(value, axis, pairs)  3.62 us
    pallas_call x1, Pallas kernels, block(): pl.pallas_call(functools.partial(conv_kernel, ngx, n), out_shape=jax.Shap...  3.21 us
    pallas_call x1, Pallas kernels, block(): pl.pallas_call(functools.partial(split_kernel, slab), out_shape=[jax.Shap...  2.04 us
    pallas_call x1, Pallas kernels, block(): pl.pallas_call(functools.partial(prepare_kernel, n, slab), out_shape=[jax...  1.57 us
  transfers between devices with their start and end apart: 21, of which 11 were waited for; matrix products, arithmetic and copies ran while one was open for 0% of the time, Pallas kernels for 8%

profile of v1, /device:TPU:17, one launch (start us, length us, event | category | flops | bytes accessed | tf_op | source)
XLA Modules:
  0.0 71.3 jit_solution(6383331987808539082)
XLA Ops:
  0.0 2.0 %shard_map.46 = (bf16[12,128,256]{2,1,0:T(8,128)(2,1)S(1)}, bf16[256,128]{1,0:T(8,128)(2,1)S(1)}, bf16[512,128]{1,0:T(8,128)(2,1)S(1)}, bf16[768,128]{1,0:T(8,12...) custom-call(bf16[3072,128]{1,0:T(8,128)(2,1)} %bitcast.3, ...), custom_call_target="tpu_custom_call" | custom-call | bytes 2359296 | tf_op jit(solution)/shard_map/pallas_call | solution.py:364
  2.0 1.3 %collective-permute-start = (bf16[768,128]{1,0:T(8,128)(2,1)S(1)}, bf16[768,128]{1,0:T(8,128)(2,1)S(1)}, u32[]{:S(2)}, u32[]{:S(2)}) collective-permute-start(bf16[768,128]{1,0:T(8,128)(2,1)S(1)} %get-tuple-element.30), channel_id=1, source_target_pairs={{0,4},{4,0},{8,12},{12,8},{16,20},{20,16},{24,28},{28,24},{1,5},{5... | collective-permute-start | bytes 589832 | tf_op jit(solution)/shard_map/ppermute | solution.py:336
  3.3 0.1 collective-permute-start.6
  3.4 1.3 %collective-permute-start.4 = (bf16[512,128]{1,0:T(8,128)(2,1)S(1)}, bf16[512,128]{1,0:T(8,128)(2,1)S(1)}, u32[]{:S(2)}, u32[]{:S(2)}) collective-permute-start(bf16[512,128]{1,0:T(8,128)(2,1)S(1)} %get-tuple-element.39), channel_id=1, source_target_pairs={{0,8},{4,12},{8,0},{12,4},{16,24},{20,28},{24,16},{28,20},{1,9},{5... | collective-permute-start | bytes 393224 | tf_op jit(solution)/shard_map/ppermute | solution.py:336
  4.7 0.1 collective-permute-start.5
  4.8 3.4 %collective-permute-done.6.refs_4_ = bf16[512,128]{1,0:T(8,128)(2,1)S(1)} collective-permute-done((bf16[512,128]{1,0:T(8,128)(2,1)S(1)}, bf16[512,128]{1,0:T(8,128)(2,1)S(1)}, u32[]{:S(2)}, u32[]{:S(2)}) %collective-permute-start.6) | collective-permute-done | bytes 131104 | tf_op jit(solution)/shard_map/ppermute | solution.py:336
  8.1 0.3 collective-permute-start.10
  8.4 5.5 %collective-permute-start.11 = (bf16[128,128]{1,0:T(8,128)(2,1)S(1)}, bf16[128,128]{1,0:T(8,128)(2,1)S(1)}, u32[]{:S(2)}, u32[]{:S(2)}) collective-permute-start(bf16[128,128]{1,0:T(8,128)(2,1)S(1)} %slice.4), channel_id=1, source_target_pairs={{0,8},{4,12},{8,0},{12,4},{16,24},{20,28},{24,16},{28,20},{1,9},{5... | collective-permute-start | bytes 98312 | tf_op jit(solution)/shard_map/ppermute | solution.py:336
  13.9 0.0 collective-permute-done.4.refs_2_
  13.9 0.9 %collective-permute-start.12 = (bf16[128,128]{1,0:T(8,128)(2,1)S(1)}, bf16[128,128]{1,0:T(8,128)(2,1)S(1)}, u32[]{:S(2)}, u32[]{:S(2)}) collective-permute-start(bf16[128,128]{1,0:T(8,128)(2,1)S(1)} %slice.4), channel_id=1, source_target_pairs={{0,12},{4,8},{8,4},{12,0},{16,28},{20,24},{24,20},{28,16},{1,13},{... | collective-permute-start | bytes 98312 | tf_op jit(solution)/shard_map/ppermute | solution.py:336
  14.9 0.0 collective-permute-done.5.refs_3_
  14.9 0.0 collective-permute-done.10.refs_5_
  14.9 0.4 collective-permute-done.11.refs_6_
  15.2 2.4 %collective-permute-done.12.refs_7_ = bf16[128,128]{1,0:T(8,128)(2,1)S(1)} collective-permute-done((bf16[128,128]{1,0:T(8,128)(2,1)S(1)}, bf16[128,128]{1,0:T(8,128)(2,1)S(1)}, u32[]{:S(2)}, u32[]{:S(2)}) %collective-permute-start.12) | collective-permute-done | bytes 32800 | tf_op jit(solution)/shard_map/ppermute | solution.py:336
  17.6 0.0 collective-permute-done.near.refs_1_
  17.6 2.3 %collective-permute-start.13 = (bf16[8,128,128]{2,1,0:T(8,128)(2,1)S(1)}, bf16[8,128,128]{2,1,0:T(8,128)(2,1)S(1)}, u32[]{:S(2)}, u32[]{:S(2)}) collective-permute-start(bf16[8,128,128]{2,1,0:T(8,128)(2,1)S(1)} %shard_map.51.mine), channel_id=1, source_target_pairs={{0,1},{1,0},{2,3},{3,2},{4,5},{5,4},{6,7},{7,6},{8,9},{9,8},{10,11... | collective-permute-start | bytes 786440 | tf_op jit(solution)/shard_map/ppermute | solution.py:336
  20.0 0.1 collective-permute-start.7
  20.1 1.7 %collective-permute-start.8 = (bf16[384,128]{1,0:T(8,128)(2,1)S(1)}, bf16[384,128]{1,0:T(8,128)(2,1)S(1)}, u32[]{:S(2)}, u32[]{:S(2)}) collective-permute-start(bf16[384,128]{1,0:T(8,128)(2,1)S(1)} %get-tuple-element.43), channel_id=1, source_target_pairs={{0,24},{4,28},{8,16},{12,20},{16,8},{20,12},{24,0},{28,4},{1,25},{... | collective-permute-start | bytes 294920 | tf_op jit(solution)/shard_map/ppermute | solution.py:336
  21.8 0.6 collective-permute-start.9
  22.4 1.6 %shard_map.48 = (bf16[64,192]{1,0:T(8,128)(2,1)S(1)}, bf16[192,64]{1,0:T(8,128)(2,1)S(1)}, bf16[6,256,256]{2,1,0:T(8,128)(2,1)S(1)}, bf16[6,256,256]{2,1,0:T(8,128)(2,1)S(1)}) custom-call(bf16[3,3,3,64,64]{4,3,2,1,0:T(8,128)(2,1)} %first.1, bf16[3,3,3,64,64]{4,3,2,1,0:T(8,128)(2,1)} %second.1), custom_call_target="tpu_custom_call" | custom-call | bytes 3538944 | tf_op jit(solution)/shard_map/pallas_call | solution.py:398
  23.9 2.1 %collective-permute-done.7.refs_5_ = bf16[384,128]{1,0:T(8,128)(2,1)S(1)} collective-permute-done((bf16[384,128]{1,0:T(8,128)(2,1)S(1)}, bf16[384,128]{1,0:T(8,128)(2,1)S(1)}, u32[]{:S(2)}, u32[]{:S(2)}) %collective-permute-start.7) | collective-permute-done | bytes 98336 | tf_op jit(solution)/shard_map/ppermute | solution.py:336
  26.1 6.9 %collective-permute-done.8.refs_6_ = bf16[384,128]{1,0:T(8,128)(2,1)S(1)} collective-permute-done((bf16[384,128]{1,0:T(8,128)(2,1)S(1)}, bf16[384,128]{1,0:T(8,128)(2,1)S(1)}, u32[]{:S(2)}, u32[]{:S(2)}) %collective-permute-start.8) | collective-permute-done | bytes 98336 | tf_op jit(solution)/shard_map/ppermute | solution.py:336
  33.0 2.4 %collective-permute-done.9.refs_7_ = bf16[384,128]{1,0:T(8,128)(2,1)S(1)} collective-permute-done((bf16[384,128]{1,0:T(8,128)(2,1)S(1)}, bf16[384,128]{1,0:T(8,128)(2,1)S(1)}, u32[]{:S(2)}, u32[]{:S(2)}) %collective-permute-start.9) | collective-permute-done | bytes 98336 | tf_op jit(solution)/shard_map/ppermute | solution.py:336
  35.5 0.0 copy-start
  35.5 0.7 %shard_map.50.coef = f32[1024,128]{1,0:T(8,128)S(1)} custom-call(bf16[64,192]{1,0:T(8,128)(2,1)S(1)} %get-tuple-element.37.basis, bf16[512,128]{1,0:T(8,128)(2,1)S(1)} %get-tuple-element.38.refs_0_, bf16[768,128]{1,0:T(8,128)(2,1)S(1)} %collective-permute-done.near.refs_1_, bf16[512,128]{1,0:T(8,128)(2,1)S(1)} %collective-permute-done.4.refs_2_, ...), custom_call_target="tpu_custom_call" | custom-call | flops 50331648 | bytes 1572864 | tf_op jit(solution)/shard_map/pallas_call | solution.py:425
  36.2 0.0 collective-permute-done.13.other
  36.2 1.3 %shard_map.52 = (bf16[384,128]{1,0:T(8,128)(2,1)S(1)}, bf16[384,128]{1,0:T(8,128)(2,1)S(1)}, bf16[384,128]{1,0:T(8,128)(2,1)S(1)}, bf16[384,128]{1,0:T(8,128)(2,...) custom-call(bf16[192,64]{1,0:T(8,128)(2,1)S(1)} %get-tuple-element.3, ...), custom_call_target="tpu_custom_call" | custom-call | flops 100663296 | bytes 1572864 | tf_op jit(solution)/shard_map/pallas_call | solution.py:434
  37.5 0.9 %collective-permute-start.14 = (bf16[384,128]{1,0:T(8,128)(2,1)S(1)}, bf16[384,128]{1,0:T(8,128)(2,1)S(1)}, u32[]{:S(2)}, u32[]{:S(2)}) collective-permute-start(bf16[384,128]{1,0:T(8,128)(2,1)S(1)} %get-tuple-element.46), channel_id=1, source_target_pairs={{0,4},{4,0},{8,12},{12,8},{16,20},{20,16},{24,28},{28,24},{1,5},{5... | collective-permute-start | bytes 294920 | tf_op jit(solution)/shard_map/ppermute | solution.py:336
  38.4 0.0 collective-permute-start.15
  38.4 2.7 %collective-permute-start.1 = (bf16[256,128]{1,0:T(8,128)(2,1)S(1)}, bf16[256,128]{1,0:T(8,128)(2,1)S(1)}, u32[]{:S(2)}, u32[]{:S(2)}) collective-permute-start(bf16[256,128]{1,0:T(8,128)(2,1)S(1)} %get-tuple-element.31), channel_id=1, source_target_pairs={{4,8},{8,4},{12,16},{16,12},{20,24},{24,20},{5,9},{9,5},{13,17},{1... | collective-permute-start | bytes 196616 | tf_op jit(solution)/shard_map/ppermute | solution.py:343
  41.2 3.2 %collective-permute-done.1.odd = bf16[256,128]{1,0:T(8,128)(2,1)S(1)} collective-permute-done((bf16[256,128]{1,0:T(8,128)(2,1)S(1)}, bf16[256,128]{1,0:T(8,128)(2,1)S(1)}, u32[]{:S(2)}, u32[]{:S(2)}) %collective-permute-start.1) | collective-permute-done | bytes 65568 | tf_op jit(solution)/shard_map/ppermute | solution.py:343
  44.4 2.4 %collective-permute-start.2 = (bf16[28,256]{1,0:T(8,128)(2,1)S(1)}, bf16[28,256]{1,0:T(8,128)(2,1)S(1)}, u32[]{:S(2)}, u32[]{:S(2)}) collective-permute-start(bf16[28,256]{1,0:T(8,128)(2,1)S(1)} %get-tuple-element.32), channel_id=1, source_target_pairs={{0,1},{1,0},{2,3},{3,2},{4,5},{5,4},{6,7},{7,6},{8,9},{9,8},{10,11... | collective-permute-start | bytes 43016 | tf_op jit(solution)/shard_map/ppermute | solution.py:336
  46.8 3.0 %collective-permute-start.3 = (bf16[28,256]{1,0:T(8,128)(2,1)S(1)}, bf16[28,256]{1,0:T(8,128)(2,1)S(1)}, u32[]{:S(2)}, u32[]{:S(2)}) collective-permute-start(bf16[28,256]{1,0:T(8,128)(2,1)S(1)} %get-tuple-element.33), channel_id=1, source_target_pairs={{1,2},{2,1},{5,6},{6,5},{9,10},{10,9},{13,14},{14,13},{17,18},{18,... | collective-permute-start | bytes 43016 | tf_op jit(solution)/shard_map/ppermute | solution.py:343
  49.9 0.1 collective-permute-start.16
  49.9 0.0 collective-permute-done.2.even_edge
  50.0 1.7 %collective-permute-start.17 = (bf16[384,128]{1,0:T(8,128)(2,1)S(1)}, bf16[384,128]{1,0:T(8,128)(2,1)S(1)}, u32[]{:S(2)}, u32[]{:S(2)}) collective-permute-start(bf16[384,128]{1,0:T(8,128)(2,1)S(1)} %get-tuple-element.49), channel_id=1, source_target_pairs={{0,16},{4,20},{8,24},{12,28},{16,0},{20,4},{24,8},{28,12},{1,17},{... | collective-permute-start | bytes 294920 | tf_op jit(solution)/shard_map/ppermute | solution.py:336
  51.7 0.5 collective-permute-done.3.odd_edge
  52.2 2.8 %collective-permute-start.18 = (bf16[384,128]{1,0:T(8,128)(2,1)S(1)}, bf16[384,128]{1,0:T(8,128)(2,1)S(1)}, u32[]{:S(2)}, u32[]{:S(2)}) collective-permute-start(bf16[384,128]{1,0:T(8,128)(2,1)S(1)} %get-tuple-element.50), channel_id=1, source_target_pairs={{0,20},{4,16},{8,28},{12,24},{16,4},{20,0},{24,12},{28,8},{1,21},{... | collective-permute-start | bytes 294920 | tf_op jit(solution)/shard_map/ppermute | solution.py:336
  54.9 0.0 collective-permute-done.14.refs_1_
  54.9 0.0 collective-permute-start.19
  55.0 0.0 collective-permute-done.15.refs_2_
  55.0 1.1 %collective-permute-start.20 = (bf16[384,128]{1,0:T(8,128)(2,1)S(1)}, bf16[384,128]{1,0:T(8,128)(2,1)S(1)}, u32[]{:S(2)}, u32[]{:S(2)}) collective-permute-start(bf16[384,128]{1,0:T(8,128)(2,1)S(1)} %get-tuple-element.52), channel_id=1, source_target_pairs={{0,28},{4,24},{8,20},{12,16},{16,12},{20,8},{24,4},{28,0},{1,29},{... | collective-permute-start | bytes 294920 | tf_op jit(solution)/shard_map/ppermute | solution.py:336
  56.1 0.0 copy-done
  56.1 3.2 %shard_map.49.base = f32[6,512,128]{2,1,0:T(8,128)S(1)} custom-call(bf16[64,48,128]{2,1,0:T(8,128)(2,1)S(1)} %bitcast.4, bf16[12,128,256]{2,1,0:T(8,128)(2,1)S(1)} %get-tuple-element.29.vt, bf16[768,128]{1,0:T(8,128)(2,1)S(1)} %collective-permute-done.near.refs_1_, bf16[256,128]{1,0:T(8,128)(2,1)S(1)} %collective-permute-done.1.odd, ...), custom_call_target="tpu_custom_call" | custom-call | flops 2415919104 | bytes 3145728 | tf_op jit(solution)/shard_map/pallas_call | solution.py:445
  59.3 0.0 collective-permute-done.16.refs_3_
  59.3 0.0 collective-permute-done.17.refs_4_
  59.3 4.5 %collective-permute-done.18.refs_5_ = bf16[384,128]{1,0:T(8,128)(2,1)S(1)} collective-permute-done((bf16[384,128]{1,0:T(8,128)(2,1)S(1)}, bf16[384,128]{1,0:T(8,128)(2,1)S(1)}, u32[]{:S(2)}, u32[]{:S(2)}) %collective-permute-start.18) | collective-permute-done | bytes 98336 | tf_op jit(solution)/shard_map/ppermute | solution.py:336
  63.7 4.1 %collective-permute-done.19.refs_6_ = bf16[384,128]{1,0:T(8,128)(2,1)S(1)} collective-permute-done((bf16[384,128]{1,0:T(8,128)(2,1)S(1)}, bf16[384,128]{1,0:T(8,128)(2,1)S(1)}, u32[]{:S(2)}, u32[]{:S(2)}) %collective-permute-start.19) | collective-permute-done | bytes 98336 | tf_op jit(solution)/shard_map/ppermute | solution.py:336
  67.9 2.2 %collective-permute-done.20.refs_7_ = bf16[384,128]{1,0:T(8,128)(2,1)S(1)} collective-permute-done((bf16[384,128]{1,0:T(8,128)(2,1)S(1)}, bf16[384,128]{1,0:T(8,128)(2,1)S(1)}, u32[]{:S(2)}, u32[]{:S(2)}) %collective-permute-start.20) | collective-permute-done | bytes 98336 | tf_op jit(solution)/shard_map/ppermute | solution.py:336
  70.1 1.3 %shard_map.53 = bf16[64,48,128]{2,1,0:T(8,128)(2,1)} custom-call(f32[6,512,128]{2,1,0:T(8,128)S(1)} %shard_map.49.base, bf16[384,128]{1,0:T(8,128)(2,1)S(1)} %get-tuple-element.45.refs_0_, bf16[384,128]{1,0:T(8,128)(2,1)S(1)} %collective-permute-done.14.refs_1_, bf16[384,128]{1,0:T(8,128)(2,1)S(1)} %collective-permute-done.15.refs_2_, ...), custom_call_target="tpu_custom_call" | custom-call | bytes 3932160 | tf_op jit(solution)/shard_map/pallas_call | solution.py:458
  (3 shorter events, 0.0 us)
Async XLA Ops:
  2.0 15.6 %collective-permute-start = (bf16[768,128]{1,0:T(8,128)(2,1)S(1)}, bf16[768,128]{1,0:T(8,128)(2,1)S(1)}, u32[]{:S(2)}, u32[]{:S(2)}) collective-permute-start(bf16[768,128]{1,0:T(8,128)(2,1)S(1)} %get-tuple-element.30), channel_id=1, source_target_pairs={{0,4},{4,0},{8,12},{12,8},{16,20},{20,16},{24,28},{28,24},{1,5},{5... | collective-permute-start | bytes 589832 | tf_op jit(solution)/shard_map/ppermute | solution.py:336
  3.3 4.8 %collective-permute-start.6 = (bf16[512,128]{1,0:T(8,128)(2,1)S(1)}, bf16[512,128]{1,0:T(8,128)(2,1)S(1)}, u32[]{:S(2)}, u32[]{:S(2)}) collective-permute-start(bf16[512,128]{1,0:T(8,128)(2,1)S(1)} %get-tuple-element.41), channel_id=1, source_target_pairs={{0,16},{4,20},{8,24},{12,28},{16,0},{20,4},{24,8},{28,12},{1,17},{... | collective-permute-start | bytes 393224 | tf_op jit(solution)/shard_map/ppermute | solution.py:336
  3.4 10.6 %collective-permute-start.4 = (bf16[512,128]{1,0:T(8,128)(2,1)S(1)}, bf16[512,128]{1,0:T(8,128)(2,1)S(1)}, u32[]{:S(2)}, u32[]{:S(2)}) collective-permute-start(bf16[512,128]{1,0:T(8,128)(2,1)S(1)} %get-tuple-element.39), channel_id=1, source_target_pairs={{0,8},{4,12},{8,0},{12,4},{16,24},{20,28},{24,16},{28,20},{1,9},{5... | collective-permute-start | bytes 393224 | tf_op jit(solution)/shard_map/ppermute | solution.py:336
  4.7 10.2 %collective-permute-start.5 = (bf16[512,128]{1,0:T(8,128)(2,1)S(1)}, bf16[512,128]{1,0:T(8,128)(2,1)S(1)}, u32[]{:S(2)}, u32[]{:S(2)}) collective-permute-start(bf16[512,128]{1,0:T(8,128)(2,1)S(1)} %get-tuple-element.40), channel_id=1, source_target_pairs={{0,12},{4,8},{8,4},{12,0},{16,28},{20,24},{24,20},{28,16},{1,13},{... | collective-permute-start | bytes 393224 | tf_op jit(solution)/shard_map/ppermute | solution.py:336
  8.1 6.7 %collective-permute-start.10 = (bf16[128,128]{1,0:T(8,128)(2,1)S(1)}, bf16[128,128]{1,0:T(8,128)(2,1)S(1)}, u32[]{:S(2)}, u32[]{:S(2)}) collective-permute-start(bf16[128,128]{1,0:T(8,128)(2,1)S(1)} %slice.4), channel_id=1, source_target_pairs={{0,4},{4,0},{8,12},{12,8},{16,20},{20,16},{24,28},{28,24},{1,5},{5... | collective-permute-start | bytes 98312 | tf_op jit(solution)/shard_map/ppermute | solution.py:336
  8.4 6.8 %collective-permute-start.11 = (bf16[128,128]{1,0:T(8,128)(2,1)S(1)}, bf16[128,128]{1,0:T(8,128)(2,1)S(1)}, u32[]{:S(2)}, u32[]{:S(2)}) collective-permute-start(bf16[128,128]{1,0:T(8,128)(2,1)S(1)} %slice.4), channel_id=1, source_target_pairs={{0,8},{4,12},{8,0},{12,4},{16,24},{20,28},{24,16},{28,20},{1,9},{5... | collective-permute-start | bytes 98312 | tf_op jit(solution)/shard_map/ppermute | solution.py:336
  13.9 3.7 %collective-permute-start.12 = (bf16[128,128]{1,0:T(8,128)(2,1)S(1)}, bf16[128,128]{1,0:T(8,128)(2,1)S(1)}, u32[]{:S(2)}, u32[]{:S(2)}) collective-permute-start(bf16[128,128]{1,0:T(8,128)(2,1)S(1)} %slice.4), channel_id=1, source_target_pairs={{0,12},{4,8},{8,4},{12,0},{16,28},{20,24},{24,20},{28,16},{1,13},{... | collective-permute-start | bytes 98312 | tf_op jit(solution)/shard_map/ppermute | solution.py:336
  17.6 18.6 %collective-permute-start.13 = (bf16[8,128,128]{2,1,0:T(8,128)(2,1)S(1)}, bf16[8,128,128]{2,1,0:T(8,128)(2,1)S(1)}, u32[]{:S(2)}, u32[]{:S(2)}) collective-permute-start(bf16[8,128,128]{2,1,0:T(8,128)(2,1)S(1)} %shard_map.51.mine), channel_id=1, source_target_pairs={{0,1},{1,0},{2,3},{3,2},{4,5},{5,4},{6,7},{7,6},{8,9},{9,8},{10,11... | collective-permute-start | bytes 786440 | tf_op jit(solution)/shard_map/ppermute | solution.py:336
  20.0 6.1 %collective-permute-start.7 = (bf16[384,128]{1,0:T(8,128)(2,1)S(1)}, bf16[384,128]{1,0:T(8,128)(2,1)S(1)}, u32[]{:S(2)}, u32[]{:S(2)}) collective-permute-start(bf16[384,128]{1,0:T(8,128)(2,1)S(1)} %get-tuple-element.42), channel_id=1, source_target_pairs={{0,20},{4,16},{8,28},{12,24},{16,4},{20,0},{24,12},{28,8},{1,21},{... | collective-permute-start | bytes 294920 | tf_op jit(solution)/shard_map/ppermute | solution.py:336
  20.1 12.9 %collective-permute-start.8 = (bf16[384,128]{1,0:T(8,128)(2,1)S(1)}, bf16[384,128]{1,0:T(8,128)(2,1)S(1)}, u32[]{:S(2)}, u32[]{:S(2)}) collective-permute-start(bf16[384,128]{1,0:T(8,128)(2,1)S(1)} %get-tuple-element.43), channel_id=1, source_target_pairs={{0,24},{4,28},{8,16},{12,20},{16,8},{20,12},{24,0},{28,4},{1,25},{... | collective-permute-start | bytes 294920 | tf_op jit(solution)/shard_map/ppermute | solution.py:336
  21.8 13.7 %collective-permute-start.9 = (bf16[384,128]{1,0:T(8,128)(2,1)S(1)}, bf16[384,128]{1,0:T(8,128)(2,1)S(1)}, u32[]{:S(2)}, u32[]{:S(2)}) collective-permute-start(bf16[384,128]{1,0:T(8,128)(2,1)S(1)} %get-tuple-element.44), channel_id=1, source_target_pairs={{0,28},{4,24},{8,20},{12,16},{16,12},{20,8},{24,4},{28,0},{1,29},{... | collective-permute-start | bytes 294920 | tf_op jit(solution)/shard_map/ppermute | solution.py:336
  35.5 20.6 %copy-start = (bf16[64,24,2,128]{3,2,1,0:T(2,128)(2,1)S(1)}, bf16[64,24,2,128]{3,2,1,0:T(2,128)(2,1)}, u32[]{:S(2)}) copy-start(bf16[64,24,2,128]{3,2,1,0:T(2,128)(2,1)} %param.4) | copy-start | bytes 2359300
  37.5 17.4 %collective-permute-start.14 = (bf16[384,128]{1,0:T(8,128)(2,1)S(1)}, bf16[384,128]{1,0:T(8,128)(2,1)S(1)}, u32[]{:S(2)}, u32[]{:S(2)}) collective-permute-start(bf16[384,128]{1,0:T(8,128)(2,1)S(1)} %get-tuple-element.46), channel_id=1, source_target_pairs={{0,4},{4,0},{8,12},{12,8},{16,20},{20,16},{24,28},{28,24},{1,5},{5... | collective-permute-start | bytes 294920 | tf_op jit(solution)/shard_map/ppermute | solution.py:336
  38.4 16.5 %collective-permute-start.15 = (bf16[384,128]{1,0:T(8,128)(2,1)S(1)}, bf16[384,128]{1,0:T(8,128)(2,1)S(1)}, u32[]{:S(2)}, u32[]{:S(2)}) collective-permute-start(bf16[384,128]{1,0:T(8,128)(2,1)S(1)} %get-tuple-element.47), channel_id=1, source_target_pairs={{0,8},{4,12},{8,0},{12,4},{16,24},{20,28},{24,16},{28,20},{1,9},{5... | collective-permute-start | bytes 294920 | tf_op jit(solution)/shard_map/ppermute | solution.py:336
  38.4 5.9 %collective-permute-start.1 = (bf16[256,128]{1,0:T(8,128)(2,1)S(1)}, bf16[256,128]{1,0:T(8,128)(2,1)S(1)}, u32[]{:S(2)}, u32[]{:S(2)}) collective-permute-start(bf16[256,128]{1,0:T(8,128)(2,1)S(1)} %get-tuple-element.31), channel_id=1, source_target_pairs={{4,8},{8,4},{12,16},{16,12},{20,24},{24,20},{5,9},{9,5},{13,17},{1... | collective-permute-start | bytes 196616 | tf_op jit(solution)/shard_map/ppermute | solution.py:343
  44.4 5.6 %collective-permute-start.2 = (bf16[28,256]{1,0:T(8,128)(2,1)S(1)}, bf16[28,256]{1,0:T(8,128)(2,1)S(1)}, u32[]{:S(2)}, u32[]{:S(2)}) collective-permute-start(bf16[28,256]{1,0:T(8,128)(2,1)S(1)} %get-tuple-element.32), channel_id=1, source_target_pairs={{0,1},{1,0},{2,3},{3,2},{4,5},{5,4},{6,7},{7,6},{8,9},{9,8},{10,11... | collective-permute-start | bytes 43016 | tf_op jit(solution)/shard_map/ppermute | solution.py:336
  46.8 5.3 %collective-permute-start.3 = (bf16[28,256]{1,0:T(8,128)(2,1)S(1)}, bf16[28,256]{1,0:T(8,128)(2,1)S(1)}, u32[]{:S(2)}, u32[]{:S(2)}) collective-permute-start(bf16[28,256]{1,0:T(8,128)(2,1)S(1)} %get-tuple-element.33), channel_id=1, source_target_pairs={{1,2},{2,1},{5,6},{6,5},{9,10},{10,9},{13,14},{14,13},{17,18},{18,... | collective-permute-start | bytes 43016 | tf_op jit(solution)/shard_map/ppermute | solution.py:343
  49.9 9.4 %collective-permute-start.16 = (bf16[384,128]{1,0:T(8,128)(2,1)S(1)}, bf16[384,128]{1,0:T(8,128)(2,1)S(1)}, u32[]{:S(2)}, u32[]{:S(2)}) collective-permute-start(bf16[384,128]{1,0:T(8,128)(2,1)S(1)} %get-tuple-element.48), channel_id=1, source_target_pairs={{0,12},{4,8},{8,4},{12,0},{16,28},{20,24},{24,20},{28,16},{1,13},{... | collective-permute-start | bytes 294920 | tf_op jit(solution)/shard_map/ppermute | solution.py:336
  50.0 9.3 %collective-permute-start.17 = (bf16[384,128]{1,0:T(8,128)(2,1)S(1)}, bf16[384,128]{1,0:T(8,128)(2,1)S(1)}, u32[]{:S(2)}, u32[]{:S(2)}) collective-permute-start(bf16[384,128]{1,0:T(8,128)(2,1)S(1)} %get-tuple-element.49), channel_id=1, source_target_pairs={{0,16},{4,20},{8,24},{12,28},{16,0},{20,4},{24,8},{28,12},{1,17},{... | collective-permute-start | bytes 294920 | tf_op jit(solution)/shard_map/ppermute | solution.py:336
  52.2 11.6 %collective-permute-start.18 = (bf16[384,128]{1,0:T(8,128)(2,1)S(1)}, bf16[384,128]{1,0:T(8,128)(2,1)S(1)}, u32[]{:S(2)}, u32[]{:S(2)}) collective-permute-start(bf16[384,128]{1,0:T(8,128)(2,1)S(1)} %get-tuple-element.50), channel_id=1, source_target_pairs={{0,20},{4,16},{8,28},{12,24},{16,4},{20,0},{24,12},{28,8},{1,21},{... | collective-permute-start | bytes 294920 | tf_op jit(solution)/shard_map/ppermute | solution.py:336
  54.9 12.9 %collective-permute-start.19 = (bf16[384,128]{1,0:T(8,128)(2,1)S(1)}, bf16[384,128]{1,0:T(8,128)(2,1)S(1)}, u32[]{:S(2)}, u32[]{:S(2)}) collective-permute-start(bf16[384,128]{1,0:T(8,128)(2,1)S(1)} %get-tuple-element.51), channel_id=1, source_target_pairs={{0,24},{4,28},{8,16},{12,20},{16,8},{20,12},{24,0},{28,4},{1,25},{... | collective-permute-start | bytes 294920 | tf_op jit(solution)/shard_map/ppermute | solution.py:336
  55.0 15.1 %collective-permute-start.20 = (bf16[384,128]{1,0:T(8,128)(2,1)S(1)}, bf16[384,128]{1,0:T(8,128)(2,1)S(1)}, u32[]{:S(2)}, u32[]{:S(2)}) collective-permute-start(bf16[384,128]{1,0:T(8,128)(2,1)S(1)} %get-tuple-element.52), channel_id=1, source_target_pairs={{0,28},{4,24},{8,20},{12,16},{16,12},{20,8},{24,4},{28,0},{1,29},{... | collective-permute-start | bytes 294920 | tf_op jit(solution)/shard_map/ppermute | solution.py:336

commit v2 on v1

--- a/solution.py
+++ b/solution.py
@@ -49,28 +49,28 @@
     half = lanes // 2
     own = weights.shape[0] // 2
     ch = weights.shape[2]
-    stride = flat.shape[0] // ch
-    ny = stride // slab
+    ny = flat.shape[1] // slab
+    deep = 4 * ny
     core = lax.axis_index("gx") % 2
     upper = lax.axis_index("depth") % 2
-    block = flat.shape[0] // 4
+    groups = pairs // 2
     loads = [
-        pltpu.make_async_copy(
-            flat.at[pl.ds(i * block, block), :], held.at[pl.ds(i * block, block), :], sem.at[i]
-        )
-        for i in range(4)
+        pltpu.make_async_copy(flat.at[:, pl.ds(deep * g, deep), :], held.at[g], sem.at[g])
+        for g in range(groups)
     ]
-    loads.append(pltpu.make_async_copy(weights.at[pl.ds(core * own, own)], modes, sem.at[4]))
+    loads.append(
+        pltpu.make_async_copy(weights.at[pl.ds(core * own, own)], modes, sem.at[groups])
+    )
     for load in loads:
         load.start()
-    for i in range(4):
-        loads[i].wait()
-        wide[pl.ds(i * block, block), :] = held[pl.ds(i * block, block), :].astype(F32)
-    for q in range(pairs):
-        rows = [wide[pl.ds(2 * q * ny + j, ch, stride=stride), :] for j in range(2 * ny)]
-        vt[q] = jnp.concatenate(rows, axis=0).astype(BF).T
+    for g in range(groups):
+        loads[g].wait()
+        wide[g] = held[g].astype(F32).reshape(deep * ch, cols)
+        for i in range(2):
+            rows = [wide[g, pl.ds(2 * ny * i + j, ch, stride=deep), :] for j in range(2 * ny)]
+            vt[2 * g + i] = jnp.concatenate(rows, axis=0).astype(BF).T
     body = 2 * pairs * part
-    loads[4].wait()
+    loads[groups].wait()
     for k in range(n):
         start = pl.multiple_of(target(k) * part, part)
         for q in range(pairs):
@@ -309,17 +309,17 @@
     part = cols // n
     half = lanes // 2
     ch = lanes // 4
-    for k in range(n):
-        start = pl.multiple_of(target(k) * part, part)
-        for q in range(pairs):
-            for par in range(2):
-                total[q, pl.ds(start, part), pl.ds(par * half, half)] = chunks[k][
-                    pl.ds((par * pairs + q) * part, part), :
-                ]
     stores = []
     for g in range(pairs // 2):
         for i in range(2):
-            turned = total[2 * g + i].T.astype(F32)
+            q = 2 * g + i
+            for k in range(n):
+                start = pl.multiple_of(target(k) * part, part)
+                for par in range(2):
+                    total[q, pl.ds(start, part), pl.ds(par * half, half)] = chunks[k][
+                        pl.ds((par * pairs + q) * part, part), :
+                    ]
+            turned = total[q].T.astype(F32)
             for j in range(4):
                 wide[g, pl.ds(4 * i + j, ch, stride=8), :] = turned[j * ch : (j + 1) * ch]
         done[g] = (base[g] + wide[g]).reshape(ch, 8, cols).astype(BF)
@@ -357,7 +357,7 @@
     wrows = mode_weights.shape[0] // 4 * ch
     total_z = slab * n
 
-    flat = volume.reshape(ch * slab * ny, cols)
+    flat = volume.reshape(ch, slab * ny, cols)
     sizes = [
         2 * per + (wrows if k <= n // 2 else 0) + (2 * cols if k == 1 else 0) for k in range(n)
     ]
@@ -371,10 +371,10 @@
         in_specs=[HBM, HBM],
         out_specs=[VMEM] * (n + 2),
         scratch_shapes=[
-            pltpu.VMEM(flat.shape, BF),
+            pltpu.VMEM((pairs // 2, ch, 4 * ny, cols), BF),
             pltpu.VMEM((mode_weights.shape[0] // 2,) + mode_weights.shape[1:], BF),
-            pltpu.VMEM(flat.shape, F32),
-            pltpu.SemaphoreType.DMA((5,)),
+            pltpu.VMEM((pairs // 2, ch * 4 * ny, cols), F32),
+            pltpu.SemaphoreType.DMA((pairs // 2 + 1,)),
         ],
         compiler_params=params(),
         cost_estimate=cost(0, 3 * volume.size * 2),
@@ -453,7 +453,7 @@
         ],
         compiler_params=params(),
         cost_estimate=cost(4 * 6 * pairs * cols * lanes * lanes, volume.size * 8),
-    )(flat.reshape(ch, slab * ny, cols), vt, got[1], odd, even_edge, odd_edge, w1, w2)
+    )(flat, vt, got[1], odd, even_edge, odd_edge, w1, w2)
 
     out = pl.pallas_call(
         join_kernel,

time: 71.5 us -> 71.3 us (level)
  no operation moved by 1% of the time
where the time goes in v2:
time: 71.3 us; the launch traced here: 71.2 us
  waiting for transfers between devices  32 us (45%)
  starting transfers between devices  29 us (41%)
  Pallas kernels  10 us (14%)
    ppermute x19, waiting for transfers between devices, swap(): lax.ppermute(value, axis, [(i, i ^ k) for i in range(count) if i ^ k < co...  28.4 us
    ppermute x19, starting transfers between devices, swap(): lax.ppermute(value, axis, [(i, i ^ k) for i in range(count) if i ^ k < co...  23.2 us
    ppermute x2, starting transfers between devices, swap_odd(): return lax.ppermute(value, axis, pairs)  5.79 us
    ppermute x2, waiting for transfers between devices, swap_odd(): return lax.ppermute(value, axis, pairs)  3.62 us
    pallas_call x1, Pallas kernels, block(): pl.pallas_call(functools.partial(conv_kernel, ngx, n), out_shape=jax.Shap...  3.21 us
    pallas_call x1, Pallas kernels, block(): pl.pallas_call(functools.partial(split_kernel, slab), out_shape=[jax.Shap...  1.91 us
    pallas_call x1, Pallas kernels, block(): pl.pallas_call(functools.partial(prepare_kernel, n, slab), out_shape=[jax...  1.57 us
  transfers between devices with their start and end apart: 21, of which 11 were waited for; matrix products, arithmetic and copies ran while one was open for 0% of the time, Pallas kernels for 8%

profile of v2, /device:TPU:17, one launch (start us, length us, event | category | flops | bytes accessed | tf_op | source)
XLA Modules:
  0.0 71.2 jit_solution(4769657585794202481)
XLA Ops:
  0.0 1.9 %shard_map.46 = (bf16[12,128,256]{2,1,0:T(8,128)(2,1)S(1)}, bf16[256,128]{1,0:T(8,128)(2,1)S(1)}, bf16[512,128]{1,0:T(8,128)(2,1)S(1)}, bf16[768,128]{1,0:T(8,12...) custom-call(bf16[64,48,128]{2,1,0:T(8,128)(2,1)} %bitcast.2, ...), custom_call_target="tpu_custom_call" | custom-call | bytes 2359296 | tf_op jit(solution)/shard_map/pallas_call | solution.py:364
  1.9 1.3 %collective-permute-start = (bf16[768,128]{1,0:T(8,128)(2,1)S(1)}, bf16[768,128]{1,0:T(8,128)(2,1)S(1)}, u32[]{:S(2)}, u32[]{:S(2)}) collective-permute-start(bf16[768,128]{1,0:T(8,128)(2,1)S(1)} %get-tuple-element.30), channel_id=1, source_target_pairs={{0,4},{4,0},{8,12},{12,8},{16,20},{20,16},{24,28},{28,24},{1,5},{5... | collective-permute-start | bytes 589832 | tf_op jit(solution)/shard_map/ppermute | solution.py:336
  3.2 0.1 collective-permute-start.6
  3.2 1.3 %collective-permute-start.4 = (bf16[512,128]{1,0:T(8,128)(2,1)S(1)}, bf16[512,128]{1,0:T(8,128)(2,1)S(1)}, u32[]{:S(2)}, u32[]{:S(2)}) collective-permute-start(bf16[512,128]{1,0:T(8,128)(2,1)S(1)} %get-tuple-element.39), channel_id=1, source_target_pairs={{0,8},{4,12},{8,0},{12,4},{16,24},{20,28},{24,16},{28,20},{1,9},{5... | collective-permute-start | bytes 393224 | tf_op jit(solution)/shard_map/ppermute | solution.py:336
  4.5 0.1 collective-permute-start.5
  4.6 3.4 %collective-permute-done.6.refs_4_ = bf16[512,128]{1,0:T(8,128)(2,1)S(1)} collective-permute-done((bf16[512,128]{1,0:T(8,128)(2,1)S(1)}, bf16[512,128]{1,0:T(8,128)(2,1)S(1)}, u32[]{:S(2)}, u32[]{:S(2)}) %collective-permute-start.6) | collective-permute-done | bytes 131104 | tf_op jit(solution)/shard_map/ppermute | solution.py:336
  8.0 0.3 collective-permute-start.10
  8.3 5.5 %collective-permute-start.11 = (bf16[128,128]{1,0:T(8,128)(2,1)S(1)}, bf16[128,128]{1,0:T(8,128)(2,1)S(1)}, u32[]{:S(2)}, u32[]{:S(2)}) collective-permute-start(bf16[128,128]{1,0:T(8,128)(2,1)S(1)} %slice.4), channel_id=1, source_target_pairs={{0,8},{4,12},{8,0},{12,4},{16,24},{20,28},{24,16},{28,20},{1,9},{5... | collective-permute-start | bytes 98312 | tf_op jit(solution)/shard_map/ppermute | solution.py:336
  13.8 0.0 collective-permute-done.4.refs_2_
  13.8 0.9 %collective-permute-start.12 = (bf16[128,128]{1,0:T(8,128)(2,1)S(1)}, bf16[128,128]{1,0:T(8,128)(2,1)S(1)}, u32[]{:S(2)}, u32[]{:S(2)}) collective-permute-start(bf16[128,128]{1,0:T(8,128)(2,1)S(1)} %slice.4), channel_id=1, source_target_pairs={{0,12},{4,8},{8,4},{12,0},{16,28},{20,24},{24,20},{28,16},{1,13},{... | collective-permute-start | bytes 98312 | tf_op jit(solution)/shard_map/ppermute | solution.py:336
  14.7 0.0 collective-permute-done.5.refs_3_
  14.7 0.0 collective-permute-done.10.refs_5_
  14.7 0.4 collective-permute-done.11.refs_6_
  15.1 2.4 %collective-permute-done.12.refs_7_ = bf16[128,128]{1,0:T(8,128)(2,1)S(1)} collective-permute-done((bf16[128,128]{1,0:T(8,128)(2,1)S(1)}, bf16[128,128]{1,0:T(8,128)(2,1)S(1)}, u32[]{:S(2)}, u32[]{:S(2)}) %collective-permute-start.12) | collective-permute-done | bytes 32800 | tf_op jit(solution)/shard_map/ppermute | solution.py:336
  17.5 0.0 collective-permute-done.near.refs_1_
  17.5 2.3 %collective-permute-start.13 = (bf16[8,128,128]{2,1,0:T(8,128)(2,1)S(1)}, bf16[8,128,128]{2,1,0:T(8,128)(2,1)S(1)}, u32[]{:S(2)}, u32[]{:S(2)}) collective-permute-start(bf16[8,128,128]{2,1,0:T(8,128)(2,1)S(1)} %shard_map.51.mine), channel_id=1, source_target_pairs={{0,1},{1,0},{2,3},{3,2},{4,5},{5,4},{6,7},{7,6},{8,9},{9,8},{10,11... | collective-permute-start | bytes 786440 | tf_op jit(solution)/shard_map/ppermute | solution.py:336
  19.8 0.1 collective-permute-start.7
  20.0 1.7 %collective-permute-start.8 = (bf16[384,128]{1,0:T(8,128)(2,1)S(1)}, bf16[384,128]{1,0:T(8,128)(2,1)S(1)}, u32[]{:S(2)}, u32[]{:S(2)}) collective-permute-start(bf16[384,128]{1,0:T(8,128)(2,1)S(1)} %get-tuple-element.43), channel_id=1, source_target_pairs={{0,24},{4,28},{8,16},{12,20},{16,8},{20,12},{24,0},{28,4},{1,25},{... | collective-permute-start | bytes 294920 | tf_op jit(solution)/shard_map/ppermute | solution.py:336
  21.7 0.6 collective-permute-start.9
  22.2 1.6 %shard_map.48 = (bf16[64,192]{1,0:T(8,128)(2,1)S(1)}, bf16[192,64]{1,0:T(8,128)(2,1)S(1)}, bf16[6,256,256]{2,1,0:T(8,128)(2,1)S(1)}, bf16[6,256,256]{2,1,0:T(8,128)(2,1)S(1)}) custom-call(bf16[3,3,3,64,64]{4,3,2,1,0:T(8,128)(2,1)} %first.1, bf16[3,3,3,64,64]{4,3,2,1,0:T(8,128)(2,1)} %second.1), custom_call_target="tpu_custom_call" | custom-call | bytes 3538944 | tf_op jit(solution)/shard_map/pallas_call | solution.py:398
  23.8 2.1 %collective-permute-done.7.refs_5_ = bf16[384,128]{1,0:T(8,128)(2,1)S(1)} collective-permute-done((bf16[384,128]{1,0:T(8,128)(2,1)S(1)}, bf16[384,128]{1,0:T(8,128)(2,1)S(1)}, u32[]{:S(2)}, u32[]{:S(2)}) %collective-permute-start.7) | collective-permute-done | bytes 98336 | tf_op jit(solution)/shard_map/ppermute | solution.py:336
  25.9 6.9 %collective-permute-done.8.refs_6_ = bf16[384,128]{1,0:T(8,128)(2,1)S(1)} collective-permute-done((bf16[384,128]{1,0:T(8,128)(2,1)S(1)}, bf16[384,128]{1,0:T(8,128)(2,1)S(1)}, u32[]{:S(2)}, u32[]{:S(2)}) %collective-permute-start.8) | collective-permute-done | bytes 98336 | tf_op jit(solution)/shard_map/ppermute | solution.py:336
  32.9 2.4 %collective-permute-done.9.refs_7_ = bf16[384,128]{1,0:T(8,128)(2,1)S(1)} collective-permute-done((bf16[384,128]{1,0:T(8,128)(2,1)S(1)}, bf16[384,128]{1,0:T(8,128)(2,1)S(1)}, u32[]{:S(2)}, u32[]{:S(2)}) %collective-permute-start.9) | collective-permute-done | bytes 98336 | tf_op jit(solution)/shard_map/ppermute | solution.py:336
  35.3 0.0 copy-start
  35.3 0.7 %shard_map.50.coef = f32[1024,128]{1,0:T(8,128)S(1)} custom-call(bf16[64,192]{1,0:T(8,128)(2,1)S(1)} %get-tuple-element.37.basis, bf16[512,128]{1,0:T(8,128)(2,1)S(1)} %get-tuple-element.38.refs_0_, bf16[768,128]{1,0:T(8,128)(2,1)S(1)} %collective-permute-done.near.refs_1_, bf16[512,128]{1,0:T(8,128)(2,1)S(1)} %collective-permute-done.4.refs_2_, ...), custom_call_target="tpu_custom_call" | custom-call | flops 50331648 | bytes 1572864 | tf_op jit(solution)/shard_map/pallas_call | solution.py:425
  36.1 0.0 collective-permute-done.13.other
  36.1 1.3 %shard_map.52 = (bf16[384,128]{1,0:T(8,128)(2,1)S(1)}, bf16[384,128]{1,0:T(8,128)(2,1)S(1)}, bf16[384,128]{1,0:T(8,128)(2,1)S(1)}, bf16[384,128]{1,0:T(8,128)(2,...) custom-call(bf16[192,64]{1,0:T(8,128)(2,1)S(1)} %get-tuple-element.3, ...), custom_call_target="tpu_custom_call" | custom-call | flops 100663296 | bytes 1572864 | tf_op jit(solution)/shard_map/pallas_call | solution.py:434
  37.4 0.9 %collective-permute-start.14 = (bf16[384,128]{1,0:T(8,128)(2,1)S(1)}, bf16[384,128]{1,0:T(8,128)(2,1)S(1)}, u32[]{:S(2)}, u32[]{:S(2)}) collective-permute-start(bf16[384,128]{1,0:T(8,128)(2,1)S(1)} %get-tuple-element.46), channel_id=1, source_target_pairs={{0,4},{4,0},{8,12},{12,8},{16,20},{20,16},{24,28},{28,24},{1,5},{5... | collective-permute-start | bytes 294920 | tf_op jit(solution)/shard_map/ppermute | solution.py:336
  38.3 0.0 collective-permute-start.15
  38.3 2.7 %collective-permute-start.1 = (bf16[256,128]{1,0:T(8,128)(2,1)S(1)}, bf16[256,128]{1,0:T(8,128)(2,1)S(1)}, u32[]{:S(2)}, u32[]{:S(2)}) collective-permute-start(bf16[256,128]{1,0:T(8,128)(2,1)S(1)} %get-tuple-element.31), channel_id=1, source_target_pairs={{4,8},{8,4},{12,16},{16,12},{20,24},{24,20},{5,9},{9,5},{13,17},{1... | collective-permute-start | bytes 196616 | tf_op jit(solution)/shard_map/ppermute | solution.py:343
  41.1 3.1 %collective-permute-done.1.odd = bf16[256,128]{1,0:T(8,128)(2,1)S(1)} collective-permute-done((bf16[256,128]{1,0:T(8,128)(2,1)S(1)}, bf16[256,128]{1,0:T(8,128)(2,1)S(1)}, u32[]{:S(2)}, u32[]{:S(2)}) %collective-permute-start.1) | collective-permute-done | bytes 65568 | tf_op jit(solution)/shard_map/ppermute | solution.py:343
  44.2 2.4 %collective-permute-start.2 = (bf16[28,256]{1,0:T(8,128)(2,1)S(1)}, bf16[28,256]{1,0:T(8,128)(2,1)S(1)}, u32[]{:S(2)}, u32[]{:S(2)}) collective-permute-start(bf16[28,256]{1,0:T(8,128)(2,1)S(1)} %get-tuple-element.32), channel_id=1, source_target_pairs={{0,1},{1,0},{2,3},{3,2},{4,5},{5,4},{6,7},{7,6},{8,9},{9,8},{10,11... | collective-permute-start | bytes 43016 | tf_op jit(solution)/shard_map/ppermute | solution.py:336
  46.7 3.0 %collective-permute-start.3 = (bf16[28,256]{1,0:T(8,128)(2,1)S(1)}, bf16[28,256]{1,0:T(8,128)(2,1)S(1)}, u32[]{:S(2)}, u32[]{:S(2)}) collective-permute-start(bf16[28,256]{1,0:T(8,128)(2,1)S(1)} %get-tuple-element.33), channel_id=1, source_target_pairs={{1,2},{2,1},{5,6},{6,5},{9,10},{10,9},{13,14},{14,13},{17,18},{18,... | collective-permute-start | bytes 43016 | tf_op jit(solution)/shard_map/ppermute | solution.py:343
  49.7 0.1 collective-permute-start.16
  49.8 0.0 collective-permute-done.2.even_edge
  49.8 1.7 %collective-permute-start.17 = (bf16[384,128]{1,0:T(8,128)(2,1)S(1)}, bf16[384,128]{1,0:T(8,128)(2,1)S(1)}, u32[]{:S(2)}, u32[]{:S(2)}) collective-permute-start(bf16[384,128]{1,0:T(8,128)(2,1)S(1)} %get-tuple-element.49), channel_id=1, source_target_pairs={{0,16},{4,20},{8,24},{12,28},{16,0},{20,4},{24,8},{28,12},{1,17},{... | collective-permute-start | bytes 294920 | tf_op jit(solution)/shard_map/ppermute | solution.py:336
  51.6 0.5 collective-permute-done.3.odd_edge
  52.0 2.8 %collective-permute-start.18 = (bf16[384,128]{1,0:T(8,128)(2,1)S(1)}, bf16[384,128]{1,0:T(8,128)(2,1)S(1)}, u32[]{:S(2)}, u32[]{:S(2)}) collective-permute-start(bf16[384,128]{1,0:T(8,128)(2,1)S(1)} %get-tuple-element.50), channel_id=1, source_target_pairs={{0,20},{4,16},{8,28},{12,24},{16,4},{20,0},{24,12},{28,8},{1,21},{... | collective-permute-start | bytes 294920 | tf_op jit(solution)/shard_map/ppermute | solution.py:336
  54.8 0.0 collective-permute-done.14.refs_1_
  54.8 0.0 collective-permute-start.19
  54.8 0.0 collective-permute-done.15.refs_2_
  54.8 1.1 %collective-permute-start.20 = (bf16[384,128]{1,0:T(8,128)(2,1)S(1)}, bf16[384,128]{1,0:T(8,128)(2,1)S(1)}, u32[]{:S(2)}, u32[]{:S(2)}) collective-permute-start(bf16[384,128]{1,0:T(8,128)(2,1)S(1)} %get-tuple-element.52), channel_id=1, source_target_pairs={{0,28},{4,24},{8,20},{12,16},{16,12},{20,8},{24,4},{28,0},{1,29},{... | collective-permute-start | bytes 294920 | tf_op jit(solution)/shard_map/ppermute | solution.py:336
  55.9 0.0 copy-done
  55.9 3.2 %shard_map.49.base = f32[6,512,128]{2,1,0:T(8,128)S(1)} custom-call(bf16[64,48,128]{2,1,0:T(8,128)(2,1)S(1)} %bitcast.3, bf16[12,128,256]{2,1,0:T(8,128)(2,1)S(1)} %get-tuple-element.29.vt, bf16[768,128]{1,0:T(8,128)(2,1)S(1)} %collective-permute-done.near.refs_1_, bf16[256,128]{1,0:T(8,128)(2,1)S(1)} %collective-permute-done.1.odd, ...), custom_call_target="tpu_custom_call" | custom-call | flops 2415919104 | bytes 3145728 | tf_op jit(solution)/shard_map/pallas_call | solution.py:445
  59.1 0.0 collective-permute-done.16.refs_3_
  59.2 0.0 collective-permute-done.17.refs_4_
  59.2 4.5 %collective-permute-done.18.refs_5_ = bf16[384,128]{1,0:T(8,128)(2,1)S(1)} collective-permute-done((bf16[384,128]{1,0:T(8,128)(2,1)S(1)}, bf16[384,128]{1,0:T(8,128)(2,1)S(1)}, u32[]{:S(2)}, u32[]{:S(2)}) %collective-permute-start.18) | collective-permute-done | bytes 98336 | tf_op jit(solution)/shard_map/ppermute | solution.py:336
  63.6 4.1 %collective-permute-done.19.refs_6_ = bf16[384,128]{1,0:T(8,128)(2,1)S(1)} collective-permute-done((bf16[384,128]{1,0:T(8,128)(2,1)S(1)}, bf16[384,128]{1,0:T(8,128)(2,1)S(1)}, u32[]{:S(2)}, u32[]{:S(2)}) %collective-permute-start.19) | collective-permute-done | bytes 98336 | tf_op jit(solution)/shard_map/ppermute | solution.py:336
  67.7 2.2 %collective-permute-done.20.refs_7_ = bf16[384,128]{1,0:T(8,128)(2,1)S(1)} collective-permute-done((bf16[384,128]{1,0:T(8,128)(2,1)S(1)}, bf16[384,128]{1,0:T(8,128)(2,1)S(1)}, u32[]{:S(2)}, u32[]{:S(2)}) %collective-permute-start.20) | collective-permute-done | bytes 98336 | tf_op jit(solution)/shard_map/ppermute | solution.py:336
  69.9 1.2 %shard_map.53 = bf16[64,48,128]{2,1,0:T(8,128)(2,1)} custom-call(f32[6,512,128]{2,1,0:T(8,128)S(1)} %shard_map.49.base, bf16[384,128]{1,0:T(8,128)(2,1)S(1)} %get-tuple-element.45.refs_0_, bf16[384,128]{1,0:T(8,128)(2,1)S(1)} %collective-permute-done.14.refs_1_, bf16[384,128]{1,0:T(8,128)(2,1)S(1)} %collective-permute-done.15.refs_2_, ...), custom_call_target="tpu_custom_call" | custom-call | bytes 3932160 | tf_op jit(solution)/shard_map/pallas_call | solution.py:458
  (3 shorter events, 0.0 us)
Async XLA Ops:
  1.9 15.6 %collective-permute-start = (bf16[768,128]{1,0:T(8,128)(2,1)S(1)}, bf16[768,128]{1,0:T(8,128)(2,1)S(1)}, u32[]{:S(2)}, u32[]{:S(2)}) collective-permute-start(bf16[768,128]{1,0:T(8,128)(2,1)S(1)} %get-tuple-element.30), channel_id=1, source_target_pairs={{0,4},{4,0},{8,12},{12,8},{16,20},{20,16},{24,28},{28,24},{1,5},{5... | collective-permute-start | bytes 589832 | tf_op jit(solution)/shard_map/ppermute | solution.py:336
  3.2 4.8 %collective-permute-start.6 = (bf16[512,128]{1,0:T(8,128)(2,1)S(1)}, bf16[512,128]{1,0:T(8,128)(2,1)S(1)}, u32[]{:S(2)}, u32[]{:S(2)}) collective-permute-start(bf16[512,128]{1,0:T(8,128)(2,1)S(1)} %get-tuple-element.41), channel_id=1, source_target_pairs={{0,16},{4,20},{8,24},{12,28},{16,0},{20,4},{24,8},{28,12},{1,17},{... | collective-permute-start | bytes 393224 | tf_op jit(solution)/shard_map/ppermute | solution.py:336
  3.2 10.6 %collective-permute-start.4 = (bf16[512,128]{1,0:T(8,128)(2,1)S(1)}, bf16[512,128]{1,0:T(8,128)(2,1)S(1)}, u32[]{:S(2)}, u32[]{:S(2)}) collective-permute-start(bf16[512,128]{1,0:T(8,128)(2,1)S(1)} %get-tuple-element.39), channel_id=1, source_target_pairs={{0,8},{4,12},{8,0},{12,4},{16,24},{20,28},{24,16},{28,20},{1,9},{5... | collective-permute-start | bytes 393224 | tf_op jit(solution)/shard_map/ppermute | solution.py:336
  4.5 10.2 %collective-permute-start.5 = (bf16[512,128]{1,0:T(8,128)(2,1)S(1)}, bf16[512,128]{1,0:T(8,128)(2,1)S(1)}, u32[]{:S(2)}, u32[]{:S(2)}) collective-permute-start(bf16[512,128]{1,0:T(8,128)(2,1)S(1)} %get-tuple-element.40), channel_id=1, source_target_pairs={{0,12},{4,8},{8,4},{12,0},{16,28},{20,24},{24,20},{28,16},{1,13},{... | collective-permute-start | bytes 393224 | tf_op jit(solution)/shard_map/ppermute | solution.py:336
  8.0 6.7 %collective-permute-start.10 = (bf16[128,128]{1,0:T(8,128)(2,1)S(1)}, bf16[128,128]{1,0:T(8,128)(2,1)S(1)}, u32[]{:S(2)}, u32[]{:S(2)}) collective-permute-start(bf16[128,128]{1,0:T(8,128)(2,1)S(1)} %slice.4), channel_id=1, source_target_pairs={{0,4},{4,0},{8,12},{12,8},{16,20},{20,16},{24,28},{28,24},{1,5},{5... | collective-permute-start | bytes 98312 | tf_op jit(solution)/shard_map/ppermute | solution.py:336
  8.3 6.8 %collective-permute-start.11 = (bf16[128,128]{1,0:T(8,128)(2,1)S(1)}, bf16[128,128]{1,0:T(8,128)(2,1)S(1)}, u32[]{:S(2)}, u32[]{:S(2)}) collective-permute-start(bf16[128,128]{1,0:T(8,128)(2,1)S(1)} %slice.4), channel_id=1, source_target_pairs={{0,8},{4,12},{8,0},{12,4},{16,24},{20,28},{24,16},{28,20},{1,9},{5... | collective-permute-start | bytes 98312 | tf_op jit(solution)/shard_map/ppermute | solution.py:336
  13.8 3.7 %collective-permute-start.12 = (bf16[128,128]{1,0:T(8,128)(2,1)S(1)}, bf16[128,128]{1,0:T(8,128)(2,1)S(1)}, u32[]{:S(2)}, u32[]{:S(2)}) collective-permute-start(bf16[128,128]{1,0:T(8,128)(2,1)S(1)} %slice.4), channel_id=1, source_target_pairs={{0,12},{4,8},{8,4},{12,0},{16,28},{20,24},{24,20},{28,16},{1,13},{... | collective-permute-start | bytes 98312 | tf_op jit(solution)/shard_map/ppermute | solution.py:336
  17.5 18.6 %collective-permute-start.13 = (bf16[8,128,128]{2,1,0:T(8,128)(2,1)S(1)}, bf16[8,128,128]{2,1,0:T(8,128)(2,1)S(1)}, u32[]{:S(2)}, u32[]{:S(2)}) collective-permute-start(bf16[8,128,128]{2,1,0:T(8,128)(2,1)S(1)} %shard_map.51.mine), channel_id=1, source_target_pairs={{0,1},{1,0},{2,3},{3,2},{4,5},{5,4},{6,7},{7,6},{8,9},{9,8},{10,11... | collective-permute-start | bytes 786440 | tf_op jit(solution)/shard_map/ppermute | solution.py:336
  19.8 6.1 %collective-permute-start.7 = (bf16[384,128]{1,0:T(8,128)(2,1)S(1)}, bf16[384,128]{1,0:T(8,128)(2,1)S(1)}, u32[]{:S(2)}, u32[]{:S(2)}) collective-permute-start(bf16[384,128]{1,0:T(8,128)(2,1)S(1)} %get-tuple-element.42), channel_id=1, source_target_pairs={{0,20},{4,16},{8,28},{12,24},{16,4},{20,0},{24,12},{28,8},{1,21},{... | collective-permute-start | bytes 294920 | tf_op jit(solution)/shard_map/ppermute | solution.py:336
  20.0 12.9 %collective-permute-start.8 = (bf16[384,128]{1,0:T(8,128)(2,1)S(1)}, bf16[384,128]{1,0:T(8,128)(2,1)S(1)}, u32[]{:S(2)}, u32[]{:S(2)}) collective-permute-start(bf16[384,128]{1,0:T(8,128)(2,1)S(1)} %get-tuple-element.43), channel_id=1, source_target_pairs={{0,24},{4,28},{8,16},{12,20},{16,8},{20,12},{24,0},{28,4},{1,25},{... | collective-permute-start | bytes 294920 | tf_op jit(solution)/shard_map/ppermute | solution.py:336
  21.7 13.7 %collective-permute-start.9 = (bf16[384,128]{1,0:T(8,128)(2,1)S(1)}, bf16[384,128]{1,0:T(8,128)(2,1)S(1)}, u32[]{:S(2)}, u32[]{:S(2)}) collective-permute-start(bf16[384,128]{1,0:T(8,128)(2,1)S(1)} %get-tuple-element.44), channel_id=1, source_target_pairs={{0,28},{4,24},{8,20},{12,16},{16,12},{20,8},{24,4},{28,0},{1,29},{... | collective-permute-start | bytes 294920 | tf_op jit(solution)/shard_map/ppermute | solution.py:336
  35.3 20.6 %copy-start = (bf16[64,24,2,128]{3,2,1,0:T(2,128)(2,1)S(1)}, bf16[64,24,2,128]{3,2,1,0:T(2,128)(2,1)}, u32[]{:S(2)}) copy-start(bf16[64,24,2,128]{3,2,1,0:T(2,128)(2,1)} %param.4) | copy-start | bytes 2359300
  37.4 17.4 %collective-permute-start.14 = (bf16[384,128]{1,0:T(8,128)(2,1)S(1)}, bf16[384,128]{1,0:T(8,128)(2,1)S(1)}, u32[]{:S(2)}, u32[]{:S(2)}) collective-permute-start(bf16[384,128]{1,0:T(8,128)(2,1)S(1)} %get-tuple-element.46), channel_id=1, source_target_pairs={{0,4},{4,0},{8,12},{12,8},{16,20},{20,16},{24,28},{28,24},{1,5},{5... | collective-permute-start | bytes 294920 | tf_op jit(solution)/shard_map/ppermute | solution.py:336
  38.3 16.5 %collective-permute-start.15 = (bf16[384,128]{1,0:T(8,128)(2,1)S(1)}, bf16[384,128]{1,0:T(8,128)(2,1)S(1)}, u32[]{:S(2)}, u32[]{:S(2)}) collective-permute-start(bf16[384,128]{1,0:T(8,128)(2,1)S(1)} %get-tuple-element.47), channel_id=1, source_target_pairs={{0,8},{4,12},{8,0},{12,4},{16,24},{20,28},{24,16},{28,20},{1,9},{5... | collective-permute-start | bytes 294920 | tf_op jit(solution)/shard_map/ppermute | solution.py:336
  38.3 5.9 %collective-permute-start.1 = (bf16[256,128]{1,0:T(8,128)(2,1)S(1)}, bf16[256,128]{1,0:T(8,128)(2,1)S(1)}, u32[]{:S(2)}, u32[]{:S(2)}) collective-permute-start(bf16[256,128]{1,0:T(8,128)(2,1)S(1)} %get-tuple-element.31), channel_id=1, source_target_pairs={{4,8},{8,4},{12,16},{16,12},{20,24},{24,20},{5,9},{9,5},{13,17},{1... | collective-permute-start | bytes 196616 | tf_op jit(solution)/shard_map/ppermute | solution.py:343
  44.2 5.6 %collective-permute-start.2 = (bf16[28,256]{1,0:T(8,128)(2,1)S(1)}, bf16[28,256]{1,0:T(8,128)(2,1)S(1)}, u32[]{:S(2)}, u32[]{:S(2)}) collective-permute-start(bf16[28,256]{1,0:T(8,128)(2,1)S(1)} %get-tuple-element.32), channel_id=1, source_target_pairs={{0,1},{1,0},{2,3},{3,2},{4,5},{5,4},{6,7},{7,6},{8,9},{9,8},{10,11... | collective-permute-start | bytes 43016 | tf_op jit(solution)/shard_map/ppermute | solution.py:336
  46.7 5.3 %collective-permute-start.3 = (bf16[28,256]{1,0:T(8,128)(2,1)S(1)}, bf16[28,256]{1,0:T(8,128)(2,1)S(1)}, u32[]{:S(2)}, u32[]{:S(2)}) collective-permute-start(bf16[28,256]{1,0:T(8,128)(2,1)S(1)} %get-tuple-element.33), channel_id=1, source_target_pairs={{1,2},{2,1},{5,6},{6,5},{9,10},{10,9},{13,14},{14,13},{17,18},{18,... | collective-permute-start | bytes 43016 | tf_op jit(solution)/shard_map/ppermute | solution.py:343
  49.7 9.4 %collective-permute-start.16 = (bf16[384,128]{1,0:T(8,128)(2,1)S(1)}, bf16[384,128]{1,0:T(8,128)(2,1)S(1)}, u32[]{:S(2)}, u32[]{:S(2)}) collective-permute-start(bf16[384,128]{1,0:T(8,128)(2,1)S(1)} %get-tuple-element.48), channel_id=1, source_target_pairs={{0,12},{4,8},{8,4},{12,0},{16,28},{20,24},{24,20},{28,16},{1,13},{... | collective-permute-start | bytes 294920 | tf_op jit(solution)/shard_map/ppermute | solution.py:336
  49.8 9.3 %collective-permute-start.17 = (bf16[384,128]{1,0:T(8,128)(2,1)S(1)}, bf16[384,128]{1,0:T(8,128)(2,1)S(1)}, u32[]{:S(2)}, u32[]{:S(2)}) collective-permute-start(bf16[384,128]{1,0:T(8,128)(2,1)S(1)} %get-tuple-element.49), channel_id=1, source_target_pairs={{0,16},{4,20},{8,24},{12,28},{16,0},{20,4},{24,8},{28,12},{1,17},{... | collective-permute-start | bytes 294920 | tf_op jit(solution)/shard_map/ppermute | solution.py:336
  52.0 11.6 %collective-permute-start.18 = (bf16[384,128]{1,0:T(8,128)(2,1)S(1)}, bf16[384,128]{1,0:T(8,128)(2,1)S(1)}, u32[]{:S(2)}, u32[]{:S(2)}) collective-permute-start(bf16[384,128]{1,0:T(8,128)(2,1)S(1)} %get-tuple-element.50), channel_id=1, source_target_pairs={{0,20},{4,16},{8,28},{12,24},{16,4},{20,0},{24,12},{28,8},{1,21},{... | collective-permute-start | bytes 294920 | tf_op jit(solution)/shard_map/ppermute | solution.py:336
  54.8 12.9 %collective-permute-start.19 = (bf16[384,128]{1,0:T(8,128)(2,1)S(1)}, bf16[384,128]{1,0:T(8,128)(2,1)S(1)}, u32[]{:S(2)}, u32[]{:S(2)}) collective-permute-start(bf16[384,128]{1,0:T(8,128)(2,1)S(1)} %get-tuple-element.51), channel_id=1, source_target_pairs={{0,24},{4,28},{8,16},{12,20},{16,8},{20,12},{24,0},{28,4},{1,25},{... | collective-permute-start | bytes 294920 | tf_op jit(solution)/shard_map/ppermute | solution.py:336
  54.8 15.1 %collective-permute-start.20 = (bf16[384,128]{1,0:T(8,128)(2,1)S(1)}, bf16[384,128]{1,0:T(8,128)(2,1)S(1)}, u32[]{:S(2)}, u32[]{:S(2)}) collective-permute-start(bf16[384,128]{1,0:T(8,128)(2,1)S(1)} %get-tuple-element.52), channel_id=1, source_target_pairs={{0,28},{4,24},{8,20},{12,16},{16,12},{20,8},{24,4},{28,0},{1,29},{... | collective-permute-start | bytes 294920 | tf_op jit(solution)/shard_map/ppermute | solution.py:336
